TPU v7x, 256 devices: a whole 4x4x8 slice. The times are simulated.
256 devices in a mesh: dp: 8 (over y, z_lo), owner: 32 (over x, z_hi, core).
Axes of the slice: x: 4, y: 4, z: 8 (z_hi: 4, z_lo: 2; z = z_hi * 2 + z_lo), core: 2. Of those that a mesh axis runs over, the one named last changes fastest.
Arguments:
- partials: bfloat16 [256, 96, 128, 128], P(('dp', 'owner')), may hold values from -1.75 to 1.75
- owners: int32 [96], replicated, may hold values from 0 to 31, as said below
- step_count: int32 [1], replicated, may hold values from 1 to 49
- master: float32 [192, 128, 128], P('owner'), may hold values from -0.3125 to 0.3125
- moment: float32 [192, 128, 128], P('owner'), may hold values from -4 to 4
- second: float32 [192, 128, 128], P('owner'), may hold values from 0.1 to 10
- stat_left: float32 [192, 128, 128], P('owner'), may hold values from -1.5 to 82
- stat_right: float32 [192, 128, 128], P('owner'), may hold values from -1.5 to 82
- basis_left: float32 [192, 128, 128], P('owner'), may hold values from -0.12 to 1.12
- basis_right: float32 [192, 128, 128], P('owner'), may hold values from -0.12 to 1.12
Outputs:
- weights_all: bfloat16 [96, 128, 128], replicated
- direction: float32 [192, 128, 128], P('owner')
- left_new: float32 [192, 128, 128], P('owner')
- right_new: float32 [192, 128, 128], P('owner')
Inputs may be any that keep to these rules, and one draw needn't show every extreme that they name: `owners`: each owner index is named by at least one and at most 6 blocks, and some index by exactly 6.
All inputs are finite; a program needn't handle non-finite values.
Results may differ from a plain program's by a relative error of at most 0.0065.
Values may be sent and summed in bfloat16 or wider, within the bound.
A program may use at most 128 MiB of HBM per device.

v0:
```python
import jax
import jax.numpy as jnp
from jax import lax
from jax.sharding import PartitionSpec as P

NS_ITERS = 6


def product(left, right):
    return jnp.matmul(left, right, precision=lax.Precision.HIGHEST)


def transposed(array):
    return jnp.swapaxes(array, 1, 2)


def refresh(stat, basis):
    power = product(stat, basis)
    magnitude = jnp.sqrt(jnp.sum(power * power, axis=(1, 2), keepdims=True))
    iterate = power / (magnitude + 1e-06)
    for repeat_count in range(NS_ITERS):
        iterate = 1.5 * iterate - 0.5 * product(iterate, product(transposed(iterate), iterate))
    return iterate


def slot_layout(owners, slot_count, total_slot_count):
    block_count = owners.shape[0]
    slot_position = jnp.arange(block_count, dtype=jnp.int32)
    before = (owners[:, None] == owners[None, :]) & (
        slot_position[:, None] > slot_position[None, :]
    )
    rank_in = jnp.sum(before.astype(jnp.int32), axis=1)
    target = owners * slot_count + rank_in
    matches = (target[:, None] == jnp.arange(total_slot_count, dtype=jnp.int32)[None, :]).astype(
        jnp.int32
    )
    source = jnp.sum(matches * slot_position[:, None], axis=0)
    occupied = jnp.sum(matches, axis=0)
    return (target, source, occupied)


def soap_update(
    gradient, occupied, moment, second, stat_left, stat_right, basis_left, basis_right, step_count
):
    elapsed = step_count[0].astype(jnp.float32)
    moment_new = 0.95 * moment + 0.05 * gradient
    rotated = product(transposed(basis_left), product(gradient, basis_right))
    rot_moment = product(transposed(basis_left), product(moment_new, basis_right))
    second_new = 0.95 * second + 0.05 * rotated * rotated
    correction = 1.0 - jnp.power(jnp.float32(0.95), elapsed)
    scaled = rot_moment / correction / (jnp.sqrt(second_new / correction) + 1e-08)
    occupied_mask = (occupied > 0)[:, None, None]
    direction = jnp.where(
        occupied_mask, product(basis_left, product(scaled, transposed(basis_right))), 0.0
    )
    left_stat = 0.95 * stat_left + 0.05 * product(gradient, transposed(gradient))
    right_stat = 0.95 * stat_right + 0.05 * product(transposed(gradient), gradient)
    left_new = jnp.where(occupied_mask, refresh(left_stat, basis_left), basis_left)
    right_new = jnp.where(occupied_mask, refresh(right_stat, basis_right), basis_right)
    return (direction, left_new, right_new)


def body(
    partials,
    owners,
    step_count,
    master,
    moment,
    second,
    stat_left,
    stat_right,
    basis_left,
    basis_right,
):
    owner_count = lax.axis_size("owner")
    slot_count = master.shape[0]
    total_slot_count = slot_count * owner_count
    target, source, occupied = slot_layout(owners, slot_count, total_slot_count)
    first_slot = lax.axis_index("owner") * slot_count
    occupied_mine = lax.dynamic_slice_in_dim(occupied, first_slot, slot_count, 0)
    own_part = partials[0]
    mask_all = (occupied > 0).astype(jnp.float32)[:, None, None]
    placed = jnp.take(own_part, source, axis=0).astype(jnp.float32) * mask_all
    summed = lax.psum_scatter(placed.astype(jnp.bfloat16), "owner", scatter_dimension=0, tiled=True)
    gradient = lax.psum(summed, "dp").astype(jnp.float32)
    direction, left_new, right_new = soap_update(
        gradient,
        occupied_mine,
        moment,
        second,
        stat_left,
        stat_right,
        basis_left,
        basis_right,
        step_count,
    )
    updated = (master - 0.01 * (direction + 0.1 * master)).astype(jnp.bfloat16)
    every_slot = lax.all_gather(updated, "owner", axis=0, tiled=True)
    weights_all = jnp.take(every_slot, target, axis=0)
    return (weights_all, direction, left_new, right_new)


def solution(mesh):
    placed = (
        P(("dp", "owner"), None, None, None),
        P(),
        P(),
        P("owner", None, None),
        P("owner", None, None),
        P("owner", None, None),
        P("owner", None, None),
        P("owner", None, None),
        P("owner", None, None),
        P("owner", None, None),
    )
    return jax.shard_map(
        body,
        mesh=mesh,
        in_specs=placed,
        out_specs=(P(), P("owner", None, None), P("owner", None, None), P("owner", None, None)),
        check_vma=False,
    )
```

profile of v0, /device:TPU:1, one launch (start us, length us, event | category | flops | bytes accessed | tf_op | source)
XLA Modules:
  0.0 320.3 jit_solution(9611837866176556709)
XLA Ops:
  9.1 8.0 %gather_fusion = bf16[192,128,128]{2,1,0:T(8,128)(2,1)} fusion(bf16[96,128,128]{2,1,0:T(8,128)(2,1)S(1)} %bitcast.85, s32[1024]{0:T(1024)S(1)} %pad_clamp_fusion.1), kind=kCustom, calls=%fused_computation | custom fusion | bytes 12583680 | tf_op jit(solution)/shard_map/jit(_take)/gather | solution.py:83
  17.1 8.6 %copy.70 = bf16[192,128,128]{1,2,0:T(8,128)(2,1)} copy(bf16[192,128,128]{2,1,0:T(8,128)(2,1)} %gather_fusion) | data formatting | bytes 12582912 | tf_op jit(solution)/shard_map/jit(_take)/gather | solution.py:83
  25.7 7.5 %multiply_convert_fusion = bf16[192,128,128]{1,2,0:T(8,128)(2,1)} fusion(f32[192]{0:T(256)S(1)} %get-tuple-element.30, bf16[192,128,128]{1,2,0:T(8,128)(2,1)} %copy.70, pred[192]{0:T(512)(128)(4,1)S(1)} %get-tuple-element.31), kind=kLoop, calls=%fused_computation.2 | loop fusion | flops 12582912 | bytes 12583872 | tf_op jit(solution)/shard_map/convert_element_type | solution.py:84
  33.3 112.5 %reduce-scatter.2.cloned.1.call-done = bf16[6,128,128]{1,2,0:T(8,128)(2,1)} async-done(((bf16[192,128,128]{1,2,0:T(8,128)(2,1)}), bf16[6,128,128]{1,2,0:T(8,128)(2,1)}) %reduce-scatter.2.cloned.1.call-update) | async-done | bytes 196624 | tf_op jit(solution)/shard_map/reduce_scatter | solution.py:84
  146.0 1.9 copy.73
  148.6 1.9 copy.69
  150.5 1.9 copy.79
  152.5 67.6 %all-reduce.2.cloned.1.call-done = bf16[6,128,128]{1,2,0:T(8,128)(2,1)} async-done(((bf16[6,128,128]{1,2,0:T(8,128)(2,1)}), bf16[6,128,128]{1,2,0:T(8,128)(2,1)}) %all-reduce.2.cloned.1.call-update) | async-done | bytes 196624 | tf_op jit(solution)/shard_map/psum | solution.py:85
  220.1 1.5 fusion.35
  221.6 1.8 fusion.22
  223.4 1.9 fusion.23
  225.3 1.5 fusion
  227.3 1.8 subtract_convert_fusion
  229.1 1.7 copy.80
  230.9 1.9 copy.92
  232.8 1.9 copy.81
  234.7 1.9 copy.102
  236.6 1.5 fusion.2
  239.0 1.5 fusion.1
  240.5 1.9 multiply_reduce_fusion.1
  259.7 1.3 fusion.11
  261.0 43.3 %all-gather.2.cloned.1.call-done = bf16[192,128,128]{2,1,0:T(8,128)(2,1)} async-done(((bf16[6,128,128]{2,1,0:T(8,128)(2,1)}), bf16[192,128,128]{2,1,0:T(8,128)(2,1)}) %all-gather.2.cloned.1.call-update) | async-done | bytes 6291472 | tf_op jit(solution)/shard_map/all_gather | solution.py:98
  304.3 5.5 %gather_fusion.1 = bf16[96,128,128]{2,1,0:T(8,128)(2,1)} fusion(bf16[192,128,128]{2,1,0:T(8,128)(2,1)} %all-gather.2.cloned.1.call-done, s32[1024]{0:T(1024)S(1)} %pad_clamp_fusion), kind=kCustom, calls=%fused_computation.1 | custom fusion | bytes 6291840 | tf_op jit(solution)/shard_map/jit(_take)/gather | solution.py:99
  309.8 3.9 %broadcast_select_fusion = bf16[96,128,128]{2,1,0:T(8,128)(2,1)} fusion(bf16[96,128,128]{2,1,0:T(8,128)(2,1)} %gather_fusion.1, pred[96]{0:T(512)(128)(4,1)S(1)} %get-tuple-element.22), kind=kLoop, calls=%fused_computation.3 | loop fusion | flops 1572864 | bytes 6291552 | tf_op jit(solution)/shard_map/jit(_take)/select_n | solution.py:99
  (52 shorter events, 20.9 us)
Async XLA Ops:
  7.2 1.9 copy-start
  7.2 138.6 %reduce-scatter.2.cloned.1.call-start = ((), (), s32[]{:S(2)}) async-start(), calls=%async_computation.1 | async-start | bytes 6488064 | tf_op jit(solution)/shard_map/reduce_scatter | solution.py:84
  33.2 186.9 %copy-start.1 = (f32[6,128,128]{2,1,0:T(8,128)S(1)}, f32[6,128,128]{2,1,0:T(8,128)}, u32[]{:S(2)}) copy-start(f32[6,128,128]{2,1,0:T(8,128)} %param.19) | copy-start | bytes 1179652
  33.2 186.8 %all-reduce.2.cloned.1.call-start = ((), (), s32[]{:S(2)}) async-start(), calls=%async_computation.2 | async-start | bytes 393216 | tf_op jit(solution)/shard_map/psum | solution.py:85
  145.8 158.6 %all-gather.2.cloned.1.call-start = ((), (), s32[]{:S(2)}) async-start(), calls=%async_computation.3 | async-start | bytes 6488064 | tf_op jit(solution)/shard_map/all_gather | solution.py:98
  220.1 7.2 %copy-start.2 = (f32[6,128,128]{2,1,0:T(8,128)S(1)}, f32[6,128,128]{2,1,0:T(8,128)}, u32[]{:S(2)}) copy-start(f32[6,128,128]{2,1,0:T(8,128)} %param.18) | copy-start | bytes 1179652
  220.1 7.2 %copy-start.4 = (f32[6,128,128]{1,2,0:T(8,128)S(1)}, f32[6,128,128]{1,2,0:T(8,128)}, u32[]{:S(2)}) copy-start(f32[6,128,128]{1,2,0:T(8,128)} %copy.79) | copy-start | bytes 1179652
  252.0 7.7 %copy-start.3 = (f32[6,128,128]{2,1,0:T(8,128)S(1)}, f32[6,128,128]{2,1,0:T(8,128)}, u32[]{:S(2)}) copy-start(f32[6,128,128]{2,1,0:T(8,128)} %param.18) | copy-start | bytes 1179652
Sparse Core Ops, SparseCore 0:
  33.3 112.3 reduce-scatter.1
  148.5 71.5 all-reduce.1
  231.0 73.2 all-gather.1
where the time goes:
time: 321 us; the launch traced here: 320 us
  waiting for transfers between devices  223 us (69%)
  local copies, waits for them, and re-layouts  35.4 us (11%)
  matrix products  33.2 us (10%)
  between operations  14.7 us (5%)
  other arithmetic  13.3 us (4%)
    reduce_scatter x1, waiting for transfers between devices, body(): lax.psum_scatter(placed.astype(jnp.bfloat16), 'owner', scatter_dimension=...  112 us
    psum x1, waiting for transfers between devices, body(): gradient = lax.psum(summed, 'dp').astype(jnp.float32)  67.6 us
    all_gather x1, waiting for transfers between devices, body(): every_slot = lax.all_gather(updated, 'owner', axis=0, tiled=True)  43.3 us
    dot_general x34, matrix products, product(): return jnp.matmul(left, right, precision=lax.Precision.HIGHEST)  33.2 us
    gather x2, local copies, waits for them, and re-layouts, body(): placed = jnp.take(own_part, source, axis=0).astype(jnp.float32) * mask_all  16.6 us
    unnamed x16, local copies, waits for them, and re-layouts  11.5 us
    convert_element_type x1, other arithmetic, body(): placed.astype(jnp.bfloat16)  7.46 us
  transfers between devices with their start and end apart: 3, of which 3 were waited for; matrix products, arithmetic and copies ran while one was open for 11% of the time, Pallas kernels for 0%

commit v1 on v0

--- a/solution.py
+++ b/solution.py
@@ -1,7 +1,13 @@
+import functools
+
 import jax
 import jax.numpy as jnp
 from jax import lax
+from jax.experimental import pallas as pl
+from jax.experimental.pallas import tpu as pltpu
 from jax.sharding import PartitionSpec as P
+
+MESH = pl.DeviceIdType.MESH
 
 NS_ITERS = 6
 
@@ -60,6 +66,46 @@
     return (direction, left_new, right_new)
 
 
+def gather_kernel(n, group, x_ref, o_ref, send_sem, recv_sem):
+    me, peer = group()
+    barrier = pltpu.get_barrier_semaphore()
+    for k in range(1, n):
+        pl.semaphore_signal(barrier, inc=1, device_id=peer(lax.rem(me + k, n)), device_id_type=MESH)
+    pl.semaphore_wait(barrier, n - 1)
+    copies = []
+    for k in range(1, n):
+        copy = pltpu.make_async_remote_copy(
+            src_ref=x_ref,
+            dst_ref=o_ref.at[me],
+            send_sem=send_sem.at[k],
+            recv_sem=recv_sem.at[k],
+            device_id=peer(lax.rem(me + k, n)),
+            device_id_type=MESH,
+        )
+        copy.start()
+        copies.append(copy)
+    o_ref[me] = x_ref[...]
+    for copy in copies:
+        copy.wait()
+
+
+def dp_group():
+    me = lax.axis_index("dp")
+    owner = lax.axis_index("owner")
+    return me, lambda j: (j, owner)
+
+
+def gather_group(x, n, group, collective_id):
+    return pl.pallas_call(
+        functools.partial(gather_kernel, n, group),
+        out_shape=jax.ShapeDtypeStruct((n,) + x.shape, x.dtype),
+        in_specs=[pl.BlockSpec(memory_space=pltpu.VMEM)],
+        out_specs=pl.BlockSpec(memory_space=pltpu.VMEM),
+        scratch_shapes=[pltpu.SemaphoreType.DMA((n,)), pltpu.SemaphoreType.DMA((n,))],
+        compiler_params=pltpu.CompilerParams(collective_id=collective_id, has_side_effects=True),
+    )(x)
+
+
 def body(
     partials,
     owners,
@@ -82,7 +128,8 @@
     mask_all = (occupied > 0).astype(jnp.float32)[:, None, None]
     placed = jnp.take(own_part, source, axis=0).astype(jnp.float32) * mask_all
     summed = lax.psum_scatter(placed.astype(jnp.bfloat16), "owner", scatter_dimension=0, tiled=True)
-    gradient = lax.psum(summed, "dp").astype(jnp.float32)
+    replicas = gather_group(summed, lax.axis_size("dp"), dp_group, 0)
+    gradient = jnp.sum(replicas.astype(jnp.float32), axis=0)
     direction, left_new, right_new = soap_update(
         gradient,
         occupied_mine,

time: 321 us -> 258 us (0.80)
  waiting for transfers between devices: 223 us -> 143 us
  Pallas kernels: 0 us -> 22.9 us
  local copies, waits for them, and re-layouts: 35.4 us -> 27.4 us
    psum x1 -> x0, waiting for transfers between devices: 67.6 us -> none  [body(): gradient = lax.psum(summed, 'dp').astype(jnp.float32)]
    pallas_call x0 -> x1, Pallas kernels: none -> 22.9 us  [gather_group(): pl.pallas_call(functools.partial(gather_kernel, n, group), out_shape=jax....]
    gather x2 -> x1, local copies, waits for them, and re-layouts: 16.6 us -> 8.02 us  [body(): placed = jnp.take(own_part, source, axis=0).astype(jnp.float32) * mask_all]
    all_gather x1, waiting for transfers between devices: 43.3 us -> 36.7 us  [body(): every_slot = lax.all_gather(updated, 'owner', axis=0, tiled=True)]
    reduce_scatter x1, waiting for transfers between devices: 112 us -> 106 us  [body(): lax.psum_scatter(placed.astype(jnp.bfloat16), 'owner', scatter_dimension=...]
    unnamed x16 -> x20, local copies, waits for them, and re-layouts: 11.5 us -> 11.3 us
  transfers between devices with their start and end apart: 3 -> 2, of which waited for: 3 -> 2; matrix products, arithmetic and copies ran while one was open for 11% -> 14% of each run, Pallas kernels for 0% -> 0%
where the time goes in v1:
time: 258 us; the launch traced here: 257 us
  waiting for transfers between devices  143 us (55%)
  matrix products  33.7 us (13%)
  local copies, waits for them, and re-layouts  27.4 us (11%)
  Pallas kernels  22.9 us (9%)
  other arithmetic  15 us (6%)
  between operations  15 us (6%)
    reduce_scatter x1, waiting for transfers between devices, body(): lax.psum_scatter(placed.astype(jnp.bfloat16), 'owner', scatter_dimension=...  106 us
    all_gather x1, waiting for transfers between devices, body(): every_slot = lax.all_gather(updated, 'owner', axis=0, tiled=True)  36.7 us
    dot_general x34, matrix products, product(): return jnp.matmul(left, right, precision=lax.Precision.HIGHEST)  33.7 us
    pallas_call x1, Pallas kernels, gather_group(): pl.pallas_call(functools.partial(gather_kernel, n, group), out_shape=jax....  22.9 us
    unnamed x20, local copies, waits for them, and re-layouts  11.3 us
    gather x1, local copies, waits for them, and re-layouts, body(): placed = jnp.take(own_part, source, axis=0).astype(jnp.float32) * mask_all  8.02 us
    convert_element_type x1, other arithmetic, body(): placed.astype(jnp.bfloat16)  7.5 us
    gather x1, local copies, waits for them, and re-layouts, body(): weights_all = jnp.take(every_slot, target, axis=0)  5.5 us
  transfers between devices with their start and end apart: 2, of which 2 were waited for; matrix products, arithmetic and copies ran while one was open for 14% of the time, Pallas kernels for 0%

profile of v1, /device:TPU:1, one launch (start us, length us, event | category | flops | bytes accessed | tf_op | source)
XLA Modules:
  0.0 257.0 jit_solution(11845315639902219849)
XLA Ops:
  7.2 1.0 convert_reduce_fusion.2
  9.1 8.0 %gather_fusion = bf16[192,128,128]{2,1,0:T(8,128)(2,1)} fusion(bf16[96,128,128]{2,1,0:T(8,128)(2,1)S(1)} %bitcast.85, s32[1024]{0:T(1024)S(1)} %pad_clamp_fusion.1), kind=kCustom, calls=%fused_computation | custom fusion | bytes 12583680 | tf_op jit(solution)/shard_map/jit(_take)/gather | solution.py:129
  17.1 7.5 %multiply_convert_fusion = bf16[192,128,128]{2,1,0:T(8,128)(2,1)} fusion(f32[192]{0:T(256)S(1)} %get-tuple-element.30, bf16[192,128,128]{2,1,0:T(8,128)(2,1)} %gather_fusion, pred[192]{0:T(512)(128)(4,1)S(1)} %get-tuple-element.31), kind=kLoop, calls=%fused_computation.2 | loop fusion | flops 12582912 | bytes 12583872 | tf_op jit(solution)/shard_map/convert_element_type | solution.py:130
  26.5 1.9 copy.69
  29.1 1.9 copy.65
  31.1 106.0 %reduce-scatter.2.cloned.1.call-done.x_ref = bf16[6,128,128]{2,1,0:T(8,128)(2,1)} async-done(((bf16[192,128,128]{2,1,0:T(8,128)(2,1)}), bf16[6,128,128]{2,1,0:T(8,128)(2,1)}) %reduce-scatter.2.cloned.1.call-update) | async-done | bytes 196624 | tf_op jit(solution)/shard_map/reduce_scatter | solution.py:130
  137.1 22.9 %shard_map.129 = bf16[8,6,128,128]{3,2,1,0:T(8,128)(2,1)} custom-call(bf16[6,128,128]{2,1,0:T(8,128)(2,1)} %reduce-scatter.2.cloned.1.call-done.x_ref), custom_call_target="tpu_custom_call" | custom-call | tf_op jit(solution)/shard_map/pallas_call | solution.py:99
  160.0 1.7 convert_reduce_fusion
  162.6 1.9 fusion.34
  164.5 2.1 fusion.23
  166.5 1.8 fusion.22
  169.4 1.8 subtract_convert_fusion
  171.2 1.7 copy.75
  173.0 1.9 copy.76
  174.9 1.9 copy.85
  176.8 1.9 copy.95
  178.7 2.0 fusion.16
  180.7 1.9 multiply_reduce_fusion.1
  182.6 1.8 fusion.8
  201.3 1.3 fusion.10
  202.7 1.3 fusion.2
  204.0 36.7 %all-gather.2.cloned.1.call-done = bf16[192,128,128]{2,1,0:T(8,128)(2,1)} async-done(((bf16[6,128,128]{2,1,0:T(8,128)(2,1)}), bf16[192,128,128]{2,1,0:T(8,128)(2,1)}) %all-gather.2.cloned.1.call-update) | async-done | bytes 6291472 | tf_op jit(solution)/shard_map/all_gather | solution.py:145
  240.7 5.5 %gather_fusion.1 = bf16[96,128,128]{2,1,0:T(8,128)(2,1)} fusion(bf16[192,128,128]{2,1,0:T(8,128)(2,1)} %all-gather.2.cloned.1.call-done, s32[1024]{0:T(1024)S(1)} %pad_clamp_fusion), kind=kCustom, calls=%fused_computation.1 | custom fusion | bytes 6291840 | tf_op jit(solution)/shard_map/jit(_take)/gather | solution.py:146
  246.2 3.9 %broadcast_select_fusion = bf16[96,128,128]{2,1,0:T(8,128)(2,1)} fusion(bf16[96,128,128]{2,1,0:T(8,128)(2,1)} %gather_fusion.1, pred[96]{0:T(512)(128)(4,1)S(1)} %get-tuple-element.22), kind=kLoop, calls=%fused_computation.4 | loop fusion | flops 1572864 | bytes 6291552 | tf_op jit(solution)/shard_map/jit(_take)/select_n | solution.py:146
  (55 shorter events, 21.6 us)
Async XLA Ops:
  7.2 1.9 copy-start
  7.2 129.9 %reduce-scatter.2.cloned.1.call-start = ((), (), s32[]{:S(2)}) async-start(), calls=%async_computation.1 | async-start | bytes 6488064 | tf_op jit(solution)/shard_map/reduce_scatter | solution.py:130
  24.6 1.0 copy-start.6
  24.6 216.1 %all-gather.2.cloned.1.call-start = ((), (), s32[]{:S(2)}) async-start(), calls=%async_computation.2 | async-start | bytes 6488064 | tf_op jit(solution)/shard_map/all_gather | solution.py:145
  162.6 5.8 %copy-start.3 = (f32[6,128,128]{2,1,0:T(8,128)S(1)}, f32[6,128,128]{2,1,0:T(8,128)}, u32[]{:S(2)}) copy-start(f32[6,128,128]{2,1,0:T(8,128)} %param.18) | copy-start | bytes 1179652
  162.6 6.3 %copy-start.1 = (f32[6,128,128]{2,1,0:T(8,128)S(1)}, f32[6,128,128]{2,1,0:T(8,128)}, u32[]{:S(2)}) copy-start(f32[6,128,128]{2,1,0:T(8,128)} %param.19) | copy-start | bytes 1179652
  164.4 5.0 %copy-start.5 = (f32[6,128,128]{1,2,0:T(8,128)S(1)}, f32[6,128,128]{1,2,0:T(8,128)}, u32[]{:S(2)}) copy-start(f32[6,128,128]{1,2,0:T(8,128)} %copy.74) | copy-start | bytes 1179652
  178.7 5.7 %copy-start.2 = (f32[6,128,128]{2,1,0:T(8,128)S(1)}, f32[6,128,128]{2,1,0:T(8,128)}, u32[]{:S(2)}) copy-start(f32[6,128,128]{2,1,0:T(8,128)} %param.19) | copy-start | bytes 1179652
  197.7 3.6 %copy-start.4 = (f32[6,128,128]{2,1,0:T(8,128)S(1)}, f32[6,128,128]{2,1,0:T(8,128)}, u32[]{:S(2)}) copy-start(f32[6,128,128]{2,1,0:T(8,128)} %param.18) | copy-start | bytes 1179652
Sparse Core Ops, SparseCore 0:
  24.8 112.2 reduce-scatter.1
  173.1 67.6 all-gather.1

commit v2 on v1

--- a/solution.py
+++ b/solution.py
@@ -66,7 +66,7 @@
     return (direction, left_new, right_new)
 
 
-def gather_kernel(n, group, x_ref, o_ref, send_sem, recv_sem):
+def group_kernel(n, group, spread, x_ref, o_ref, send_sem, recv_sem):
     me, peer = group()
     barrier = pltpu.get_barrier_semaphore()
     for k in range(1, n):
@@ -74,17 +74,18 @@
     pl.semaphore_wait(barrier, n - 1)
     copies = []
     for k in range(1, n):
+        other = lax.rem(me + k, n)
         copy = pltpu.make_async_remote_copy(
-            src_ref=x_ref,
+            src_ref=x_ref.at[other] if spread else x_ref,
             dst_ref=o_ref.at[me],
             send_sem=send_sem.at[k],
             recv_sem=recv_sem.at[k],
-            device_id=peer(lax.rem(me + k, n)),
+            device_id=peer(other),
             device_id_type=MESH,
         )
         copy.start()
         copies.append(copy)
-    o_ref[me] = x_ref[...]
+    o_ref[me] = x_ref[me] if spread else x_ref[...]
     for copy in copies:
         copy.wait()
 
@@ -95,15 +96,56 @@
     return me, lambda j: (j, owner)
 
 
-def gather_group(x, n, group, collective_id):
+def core_group():
+    replica = lax.axis_index("dp")
+    owner = lax.axis_index("owner")
+    me = lax.rem(owner, 2)
+    return me, lambda j: (replica, owner - me + j)
+
+
+def chip_group():
+    replica = lax.axis_index("dp")
+    owner = lax.axis_index("owner")
+    core = lax.rem(owner, 2)
+    return lax.div(owner, 2), lambda j: (replica, j * 2 + core)
+
+
+GROUPS = {"dp": dp_group, "core": core_group, "chip": chip_group}
+CALLS = []
+
+
+def exchange(x, name, n, spread):
+    CALLS.append(name)
+    shape = x.shape[1:] if spread else x.shape
     return pl.pallas_call(
-        functools.partial(gather_kernel, n, group),
-        out_shape=jax.ShapeDtypeStruct((n,) + x.shape, x.dtype),
+        functools.partial(group_kernel, n, GROUPS[name], spread),
+        out_shape=jax.ShapeDtypeStruct((n,) + shape, x.dtype),
         in_specs=[pl.BlockSpec(memory_space=pltpu.VMEM)],
         out_specs=pl.BlockSpec(memory_space=pltpu.VMEM),
         scratch_shapes=[pltpu.SemaphoreType.DMA((n,)), pltpu.SemaphoreType.DMA((n,))],
-        compiler_params=pltpu.CompilerParams(collective_id=collective_id, has_side_effects=True),
+        compiler_params=pltpu.CompilerParams(
+            collective_id=len(CALLS) - 1, has_side_effects=True, vmem_limit_bytes=48 * 1024 * 1024
+        ),
     )(x)
+
+
+def reduce_in(x, name, n):
+    return jnp.sum(exchange(x, name, n, True).astype(jnp.float32), axis=0)
+
+
+def all_reduce_blocks(blocks, n_dp, n_chip):
+    count, rows, cols = blocks.shape
+    per = count // (2 * n_dp)
+    half = reduce_in(blocks.reshape(2, count // 2, rows, cols), "core", 2).astype(jnp.bfloat16)
+    mine = reduce_in(half.reshape(n_dp, per, rows, cols), "dp", n_dp).astype(jnp.bfloat16)
+    piece = reduce_in(mine.reshape(n_chip, per * rows // n_chip, cols), "chip", n_chip)
+    return spread_out(piece.astype(jnp.bfloat16), n_dp, n_chip, per, rows, cols)
+
+
+def spread_out(piece, n_dp, n_chip, per, rows, cols):
+    mine = exchange(piece, "chip", n_chip, False).reshape(per, rows, cols)
+    half = exchange(mine, "dp", n_dp, False).reshape(n_dp * per, rows, cols)
+    return exchange(half, "core", 2, False).reshape(2 * n_dp * per, rows, cols)
 
 
 def body(
@@ -118,18 +160,19 @@
     basis_left,
     basis_right,
 ):
+    CALLS.clear()
     owner_count = lax.axis_size("owner")
+    n_dp = lax.axis_size("dp")
+    n_chip = owner_count // 2
     slot_count = master.shape[0]
     total_slot_count = slot_count * owner_count
     target, source, occupied = slot_layout(owners, slot_count, total_slot_count)
     first_slot = lax.axis_index("owner") * slot_count
     occupied_mine = lax.dynamic_slice_in_dim(occupied, first_slot, slot_count, 0)
-    own_part = partials[0]
-    mask_all = (occupied > 0).astype(jnp.float32)[:, None, None]
-    placed = jnp.take(own_part, source, axis=0).astype(jnp.float32) * mask_all
-    summed = lax.psum_scatter(placed.astype(jnp.bfloat16), "owner", scatter_dimension=0, tiled=True)
-    replicas = gather_group(summed, lax.axis_size("dp"), dp_group, 0)
-    gradient = jnp.sum(replicas.astype(jnp.float32), axis=0)
+    source_mine = lax.dynamic_slice_in_dim(source, first_slot, slot_count, 0)
+    grad_sum = all_reduce_blocks(partials[0], n_dp, n_chip)
+    mask_mine = (occupied_mine > 0).astype(jnp.float32)[:, None, None]
+    gradient = jnp.take(grad_sum, source_mine, axis=0).astype(jnp.float32) * mask_mine
     direction, left_new, right_new = soap_update(
         gradient,
         occupied_mine,
@@ -142,8 +185,20 @@
         step_count,
     )
     updated = (master - 0.01 * (direction + 0.1 * master)).astype(jnp.bfloat16)
-    every_slot = lax.all_gather(updated, "owner", axis=0, tiled=True)
-    weights_all = jnp.take(every_slot, target, axis=0)
+    block_count = owners.shape[0]
+    count, rows, cols = block_count, updated.shape[1], updated.shape[2]
+    per = count // (2 * n_dp)
+    rank = target - first_slot
+    in_mine = (rank >= 0) & (rank < slot_count)
+    dense = jnp.where(
+        in_mine[:, None, None], jnp.take(updated, jnp.clip(rank, 0, slot_count - 1), axis=0), 0
+    ).astype(jnp.bfloat16)
+    replica = lax.axis_index("dp")
+    chunks = dense.reshape(2, n_dp, per, rows, cols)
+    chunks = lax.dynamic_index_in_dim(chunks, replica, axis=1, keepdims=False)
+    pair = reduce_in(chunks, "core", 2)
+    piece = reduce_in(pair.astype(jnp.bfloat16).reshape(n_chip, per * rows // n_chip, cols), "chip", n_chip)
+    weights_all = spread_out(piece.astype(jnp.bfloat16), n_dp, n_chip, per, rows, cols)
     return (weights_all, direction, left_new, right_new)
 
 

time: 258 us -> 190 us (0.74)
  waiting for transfers between devices: 143 us -> 0 us
  Pallas kernels: 22.9 us -> 131 us
  between operations: 15 us -> 1.85 us
  other arithmetic: 15 us -> 5.74 us
  local copies, waits for them, and re-layouts: 27.4 us -> 18.7 us
    pallas_call x1 -> x11, Pallas kernels: 22.9 us -> 131 us  [exchange(): pl.pallas_call(functools.partial(group_kernel, n, GROUPS[name], spread),...]
    reduce_scatter x1 -> x0, waiting for transfers between devices: 106 us -> none  [body(): lax.psum_scatter(placed.astype(jnp.bfloat16), 'owner', scatter_dimension=...]
    all_gather x1 -> x0, waiting for transfers between devices: 36.7 us -> none  [body(): every_slot = lax.all_gather(updated, 'owner', axis=0, tiled=True)]
    gather x2 -> x3, local copies, waits for them, and re-layouts: 13.5 us -> 5.13 us  [the longest x1 2.72 us: body(): jnp.take(updated, jnp.clip(rank, 0, slot_count - 1), axis=0)]
    convert_element_type x2 -> x0, other arithmetic: 7.51 us -> none  [the longest x1 7.5 us: body(): placed.astype(jnp.bfloat16)]
    select_n x3 -> x0, other arithmetic: 3.91 us -> none  [the longest x2 3.91 us: body(): weights_all = jnp.take(every_slot, target, axis=0)]
    unnamed x20 -> x32, local copies, waits for them, and re-layouts: 11.3 us -> 12.3 us
  transfers between devices with their start and end apart: 2 -> 0, of which waited for: 2 -> 0; matrix products, arithmetic and copies ran while one was open for 14% -> 0% of each run, Pallas kernels for 0% -> 0%
where the time goes in v2:
time: 190 us
  Pallas kernels  131 us (69%)
  matrix products  32 us (17%)
  local copies, waits for them, and re-layouts  18.7 us (10%)
  other arithmetic  5.74 us (3%)
    pallas_call x11, Pallas kernels, exchange(): pl.pallas_call(functools.partial(group_kernel, n, GROUPS[name], spread),...  131 us
    dot_general x34, matrix products, product(): return jnp.matmul(left, right, precision=lax.Precision.HIGHEST)  32 us
    unnamed x32, local copies, waits for them, and re-layouts  12.3 us

profile of v2, /device:TPU:1, one launch (start us, length us, event | category | flops | bytes accessed | tf_op | source)
XLA Modules:
  0.0 189.5 jit_solution(10856774712628964637)
XLA Ops:
  0.6 1.9 %copy.51 = f32[6,128,128]{1,2,0:T(8,128)} copy(f32[6,128,128]{2,1,0:T(8,128)} %param.13) | data formatting | bytes 786432 | tf_op args[3]
  5.4 8.2 %shard_map.129 = bf16[2,48,128,128]{3,2,1,0:T(8,128)(2,1)S(1)} custom-call(bf16[2,48,128,128]{3,2,1,0:T(8,128)(2,1)} %bitcast.100), custom_call_target="tpu_custom_call" | custom-call | tf_op jit(solution)/shard_map/pallas_call | solution.py:120
  13.6 2.3 %reduce_sum.108 = bf16[48,128,128]{2,1,0:T(8,128)(2,1)} reduce(bf16[2,48,128,128]{3,2,1,0:T(8,128)(2,1)S(1)} %shard_map.129, bf16[]{:T(256)} %constant.46.clone.1), dimensions={0}, to_apply=%region_3.0 | reduce | flops 786432 | bytes 4718594 | tf_op jit(solution)/shard_map/reduce_sum | solution.py:133
  15.9 1.4 copy-done
  17.3 21.4 %shard_map.130 = bf16[8,6,128,128]{3,2,1,0:T(8,128)(2,1)S(1)} custom-call(bf16[8,6,128,128]{3,2,1,0:T(8,128)(2,1)S(1)} %bitcast.91), custom_call_target="tpu_custom_call" | custom-call | tf_op jit(solution)/shard_map/pallas_call | solution.py:120
  39.0 14.1 %shard_map.131 = bf16[16,48,128]{2,1,0:T(8,128)(2,1)S(1)} custom-call(bf16[16,48,128]{2,1,0:T(8,128)(2,1)S(1)} %bitcast.98), custom_call_target="tpu_custom_call" | custom-call | tf_op jit(solution)/shard_map/pallas_call | solution.py:120
  53.1 10.7 %shard_map.132 = bf16[16,48,128]{2,1,0:T(8,128)(2,1)S(1)} custom-call(bf16[48,128]{1,0:T(8,128)(2,1)S(1)} %reduce_sum.110.x_ref), custom_call_target="tpu_custom_call" | custom-call | tf_op jit(solution)/shard_map/pallas_call | solution.py:120
  63.8 20.6 %shard_map.133 = bf16[8,6,128,128]{3,2,1,0:T(8,128)(2,1)S(1)} custom-call(bf16[6,128,128]{2,1,0:T(8,128)(2,1)S(1)} %bitcast.95), custom_call_target="tpu_custom_call" | custom-call | tf_op jit(solution)/shard_map/pallas_call | solution.py:120
  84.5 4.6 %shard_map.134 = bf16[2,48,128,128]{3,2,1,0:T(8,128)(2,1)S(1)} custom-call(bf16[48,128,128]{2,1,0:T(8,128)(2,1)S(1)} %bitcast.92), custom_call_target="tpu_custom_call" | custom-call | tf_op jit(solution)/shard_map/pallas_call | solution.py:120
  94.2 1.7 fusion.22
  98.1 1.7 subtract_convert_fusion
  99.8 2.7 %gather_fusion.1 = bf16[96,128,128]{1,2,0:T(8,128)(2,1)} fusion(bf16[6,128,128]{1,2,0:T(8,128)(2,1)S(1)} %get-tuple-element.25, s32[1024]{0:T(1024)S(1)} %pad_clamp_fusion), kind=kCustom, calls=%fused_computation.1 | custom fusion | bytes 6291840 | tf_op jit(solution)/shard_map/jit(_take)/gather | solution.py:194
  104.2 1.6 shard_map.135
  105.9 10.9 %shard_map.136 = bf16[16,48,128]{2,1,0:T(8,128)(2,1)S(1)} custom-call(bf16[16,48,128]{2,1,0:T(8,128)(2,1)S(1)} %bitcast.97), custom_call_target="tpu_custom_call" | custom-call | tf_op jit(solution)/shard_map/pallas_call | solution.py:120
  116.8 11.5 %shard_map.137 = bf16[16,48,128]{2,1,0:T(8,128)(2,1)S(1)} custom-call(bf16[48,128]{1,0:T(8,128)(2,1)S(1)} %reduce_sum.112.x_ref), custom_call_target="tpu_custom_call" | custom-call | tf_op jit(solution)/shard_map/pallas_call | solution.py:120
  128.4 24.0 %shard_map.138 = bf16[8,6,128,128]{3,2,1,0:T(8,128)(2,1)S(1)} custom-call(bf16[6,128,128]{2,1,0:T(8,128)(2,1)S(1)} %bitcast.96), custom_call_target="tpu_custom_call" | custom-call | tf_op jit(solution)/shard_map/pallas_call | solution.py:120
  152.4 3.7 %shard_map.139 = bf16[2,48,128,128]{3,2,1,0:T(8,128)(2,1)S(1)} custom-call(bf16[48,128,128]{2,1,0:T(8,128)(2,1)S(1)} %bitcast.93), custom_call_target="tpu_custom_call" | custom-call | tf_op jit(solution)/shard_map/pallas_call | solution.py:120
  156.1 1.9 %copy.74 = f32[6,128,128]{2,1,0:T(8,128)} copy(f32[6,128,128]{1,2,0:T(8,128)} %get-tuple-element.26) | data formatting | bytes 786432
  158.1 1.9 %copy.53 = f32[6,128,128]{1,2,0:T(8,128)} copy(f32[6,128,128]{2,1,0:T(8,128)} %param.16) | data formatting | bytes 786432 | tf_op args[6]
  160.0 2.3 %fusion.16 = f32[6,128,128]{1,2,0:T(8,128)S(1)} fusion(f32[6,128,128]{1,2,0:T(8,128)} %copy.53, f32[6]{0:T(128)S(1)} %get-tuple-element.31, bf16[6,128,128]{1,2,0:T(8,128)(2,1)} %copy-done.4, pred[6]{0:T(512)(128)(4,1)S(1)} %get-tuple-element.21), kind=kOutput, calls=%fused_computation.34 | convolution fusion | flops 151584768 | bytes 983070 | tf_op jit(solution)/shard_map/dot_general | solution.py:16
  162.2 1.9 %multiply_reduce_fusion.1 = (f32[6]{0:T(128)S(1)}, f32[6,128,128]{2,1,0:T(8,128)S(1)}) fusion(f32[6,128,128]{1,2,0:T(8,128)S(1)} %fusion.16, f32[6,128,128]{2,1,0:T(8,128)} %param.18), kind=kOutput, calls=%fused_computation.44 | convolution fusion | flops 151191552 | bytes 1179672 | tf_op jit(solution)/shard_map/dot_general | solution.py:16
  173.4 1.9 %copy.64 = f32[6,128,128]{1,2,0:T(8,128)} copy(f32[6,128,128]{2,1,0:T(8,128)} %param.17) | data formatting | bytes 786432 | tf_op args[7]
  175.3 2.3 %fusion.8 = f32[6,128,128]{1,2,0:T(8,128)S(1)} fusion(f32[6,128,128]{1,2,0:T(8,128)} %copy.64, f32[6]{0:T(128)S(1)} %get-tuple-element.31, bf16[6,128,128]{1,2,0:T(8,128)(2,1)} %copy-done.4, pred[6]{0:T(512)(128)(4,1)S(1)} %get-tuple-element.21), kind=kOutput, calls=%fused_computation.19 | convolution fusion | flops 151584768 | bytes 983070 | tf_op jit(solution)/shard_map/dot_general | solution.py:16
  187.9 1.7 copy.103
  (77 shorter events, 30.8 us)
Async XLA Ops:
  4.7 8.9 %copy-start.8 = (s32[96]{0:T(128)}, s32[96]{0:T(128)S(1)}, u32[]{:S(2)}) copy-start(s32[96]{0:T(128)S(1)} %get-tuple-element.20) | copy-start | bytes 1156
  15.9 1.4 copy-start
  63.8 25.2 %copy-start.7 = (s32[6]{0:T(128)S(1)}, s32[6]{0:T(128)}, u32[]{:S(2)}) copy-start(s32[6]{0:T(128)} %get-tuple-element.22) | copy-start | bytes 76
  84.5 7.0 %copy-start.1 = (f32[6,128,128]{2,1,0:T(8,128)S(1)}, f32[6,128,128]{2,1,0:T(8,128)}, u32[]{:S(2)}) copy-start(f32[6,128,128]{2,1,0:T(8,128)} %param.19) | copy-start | bytes 1179652
  90.3 5.6 %copy-start.6 = (f32[6,128,128]{2,1,0:T(8,128)S(1)}, f32[6,128,128]{2,1,0:T(8,128)}, u32[]{:S(2)}) copy-start(f32[6,128,128]{2,1,0:T(8,128)} %param.14) | copy-start | bytes 1179652
  90.3 6.7 %copy-start.2 = (f32[6,128,128]{2,1,0:T(8,128)S(1)}, f32[6,128,128]{2,1,0:T(8,128)}, u32[]{:S(2)}) copy-start(f32[6,128,128]{2,1,0:T(8,128)} %param.18) | copy-start | bytes 1179652
  91.5 6.1 %copy-start.4 = (bf16[6,128,128]{1,2,0:T(8,128)(2,1)}, bf16[6,128,128]{1,2,0:T(8,128)(2,1)S(1)}, u32[]{:S(2)}) copy-start(bf16[6,128,128]{1,2,0:T(8,128)(2,1)S(1)} %copy.42) | copy-start | bytes 589828
  94.2 3.9 %copy-start.5 = (f32[6,128,128]{1,2,0:T(8,128)S(1)}, f32[6,128,128]{1,2,0:T(8,128)}, u32[]{:S(2)}) copy-start(f32[6,128,128]{1,2,0:T(8,128)} %copy.51) | copy-start | bytes 1179652
  96.1 3.7 %copy-start.11 = (s32[96]{0:T(128)S(1)}, s32[96]{0:T(128)}, u32[]{:S(2)}) copy-start(s32[96]{0:T(128)} %get-tuple-element.19) | copy-start | bytes 1156
  99.8 4.0 %copy-start.10 = (pred[96]{0:T(512)(128)(4,1)S(1)}, pred[96]{0:T(512)(128)(4,1)}, u32[]{:S(2)}) copy-start(pred[96]{0:T(512)(128)(4,1)} %get-tuple-element.18) | copy-start | bytes 292
  99.8 4.1 %copy-start.9 = (s32[96]{0:T(128)S(1)}, s32[96]{0:T(128)}, u32[]{:S(2)}) copy-start(s32[96]{0:T(128)} %copy-done.8) | copy-start | bytes 1156
  168.4 3.6 %copy-start.3 = (f32[6,128,128]{2,1,0:T(8,128)S(1)}, f32[6,128,128]{2,1,0:T(8,128)}, u32[]{:S(2)}) copy-start(f32[6,128,128]{2,1,0:T(8,128)} %param.18) | copy-start | bytes 1179652

commit v3 on v0

--- a/solution.py
+++ b/solution.py
@@ -1,7 +1,13 @@
+import functools
+
 import jax
 import jax.numpy as jnp
 from jax import lax
+from jax.experimental import pallas as pl
+from jax.experimental.pallas import tpu as pltpu
 from jax.sharding import PartitionSpec as P
+
+MESH = pl.DeviceIdType.MESH
 
 NS_ITERS = 6
 
@@ -60,6 +66,181 @@
     return (direction, left_new, right_new)
 
 
+def dp_group():
+    me = lax.axis_index("dp")
+    owner = lax.axis_index("owner")
+    return me, lambda j: (j, owner)
+
+
+def core_group():
+    replica = lax.axis_index("dp")
+    owner = lax.axis_index("owner")
+    me = lax.rem(owner, 2)
+    return me, lambda j: (replica, owner - me + j)
+
+
+def chip_group():
+    replica = lax.axis_index("dp")
+    owner = lax.axis_index("owner")
+    core = lax.rem(owner, 2)
+    return lax.div(owner, 2), lambda j: (replica, j * 2 + core)
+
+
+def enter(groups):
+    barrier = pltpu.get_barrier_semaphore()
+    total = 0
+    for n, me, peer in groups:
+        for k in range(1, n):
+            pl.semaphore_signal(barrier, inc=1, device_id=peer(lax.rem(me + k, n)), device_id_type=MESH)
+        total += n - 1
+    pl.semaphore_wait(barrier, total)
+
+
+def phase(group, source, dest, send, recv):
+    n, me, peer = group
+    copies = []
+    for k in range(1, n):
+        other = lax.rem(me + k, n)
+        copy = pltpu.make_async_remote_copy(
+            src_ref=source(other),
+            dst_ref=dest(me),
+            send_sem=send.at[k],
+            recv_sem=recv.at[k],
+            device_id=peer(other),
+            device_id_type=MESH,
+        )
+        copy.start()
+        copies.append(copy)
+    return copies
+
+
+def finish(copies):
+    for copy in copies:
+        copy.wait()
+
+
+def sum_slots(buf, out, n, rows, start):
+    step = 128 if rows % 128 == 0 else rows
+
+    def one(i, carry):
+        at = pl.multiple_of(i * step, step)
+        total = buf[0, pl.ds(at, step), :].astype(jnp.float32)
+        for j in range(1, n):
+            total = total + buf[j, pl.ds(at, step), :].astype(jnp.float32)
+        out[pl.ds(start + at, step), :] = total.astype(out.dtype)
+        return carry
+
+    lax.fori_loop(0, rows // step, one, 0)
+
+
+def spread_phases(o_ref, core, dp, chip, piece, send, recv, first):
+    n_dp, n_chip = dp[0], chip[0]
+    c, r, m = core[1], dp[1], chip[1]
+    chunk = n_chip * piece
+    half = n_dp * chunk
+    base = c * half + r * chunk
+    finish(phase(chip, lambda j: o_ref.at[pl.ds(base + m * piece, piece)],
+                 lambda me: o_ref.at[pl.ds(base + me * piece, piece)], send.at[first], recv.at[first]))
+    finish(phase(dp, lambda j: o_ref.at[pl.ds(c * half + r * chunk, chunk)],
+                 lambda me: o_ref.at[pl.ds(c * half + me * chunk, chunk)], send.at[first + 1], recv.at[first + 1]))
+    finish(phase(core, lambda j: o_ref.at[pl.ds(c * half, half)],
+                 lambda me: o_ref.at[pl.ds(me * half, half)], send.at[first + 2], recv.at[first + 2]))
+
+
+def groups_of(n_dp, n_chip):
+    core_me, core_peer = core_group()
+    dp_me, dp_peer = dp_group()
+    chip_me, chip_peer = chip_group()
+    return (2, core_me, core_peer), (n_dp, dp_me, dp_peer), (n_chip, chip_me, chip_peer)
+
+
+def grad_kernel(n_dp, n_chip, p_ref, o_ref, buf1, hbuf, buf2, mbuf, buf3, send, recv):
+    core, dp, chip = groups_of(n_dp, n_chip)
+    enter((core, dp, chip))
+    half = p_ref.shape[0] // 2
+    chunk = half // n_dp
+    piece = chunk // n_chip
+    c, r, m = core[1], dp[1], chip[1]
+    finish(phase(core, lambda j: p_ref.at[pl.ds(j * half, half)], lambda me: buf1.at[1], send.at[0], recv.at[0]))
+    buf1[0] = p_ref[pl.ds(c * half, half), :]
+    sum_slots(buf1, hbuf, 2, half, 0)
+    buf2[r] = hbuf[pl.ds(r * chunk, chunk), :]
+    finish(phase(dp, lambda j: hbuf.at[pl.ds(j * chunk, chunk)], lambda me: buf2.at[me], send.at[1], recv.at[1]))
+    sum_slots(buf2, mbuf, n_dp, chunk, 0)
+    buf3[m] = mbuf[pl.ds(m * piece, piece), :]
+    finish(phase(chip, lambda j: mbuf.at[pl.ds(j * piece, piece)], lambda me: buf3.at[me], send.at[2], recv.at[2]))
+    sum_slots(buf3, o_ref, n_chip, piece, c * half + r * chunk + m * piece)
+    spread_phases(o_ref, core, dp, chip, piece, send, recv, 3)
+
+
+def weight_kernel(n_dp, n_chip, x_ref, o_ref, buf1, pbuf, buf3, send, recv):
+    core, dp, chip = groups_of(n_dp, n_chip)
+    enter((core, dp, chip))
+    chunk = x_ref.shape[1]
+    piece = chunk // n_chip
+    half = n_dp * chunk
+    c, r, m = core[1], dp[1], chip[1]
+    finish(phase(core, lambda j: x_ref.at[j], lambda me: buf1.at[1], send.at[0], recv.at[0]))
+    buf1[0] = x_ref[c]
+    sum_slots(buf1, pbuf, 2, chunk, 0)
+    buf3[m] = pbuf[pl.ds(m * piece, piece), :]
+    finish(phase(chip, lambda j: pbuf.at[pl.ds(j * piece, piece)], lambda me: buf3.at[me], send.at[1], recv.at[1]))
+    sum_slots(buf3, o_ref, n_chip, piece, c * half + r * chunk + m * piece)
+    spread_phases(o_ref, core, dp, chip, piece, send, recv, 2)
+
+
+def params(collective_id):
+    return pltpu.CompilerParams(
+        collective_id=collective_id, has_side_effects=True, vmem_limit_bytes=48 * 1024 * 1024
+    )
+
+
+def all_reduce_blocks(blocks, n_dp, n_chip):
+    count, rows, cols = blocks.shape
+    flat = blocks.reshape(count * rows, cols)
+    half = count * rows // 2
+    chunk = half // n_dp
+    piece = chunk // n_chip
+    vmem = pl.BlockSpec(memory_space=pltpu.VMEM)
+    out = pl.pallas_call(
+        functools.partial(grad_kernel, n_dp, n_chip),
+        out_shape=jax.ShapeDtypeStruct(flat.shape, flat.dtype),
+        in_specs=[vmem],
+        out_specs=vmem,
+        scratch_shapes=[
+            pltpu.VMEM((2, half, cols), flat.dtype),
+            pltpu.VMEM((half, cols), flat.dtype),
+            pltpu.VMEM((n_dp, chunk, cols), flat.dtype),
+            pltpu.VMEM((chunk, cols), flat.dtype),
+            pltpu.VMEM((n_chip, piece, cols), flat.dtype),
+            pltpu.SemaphoreType.DMA((6, n_chip)),
+            pltpu.SemaphoreType.DMA((6, n_chip)),
+        ],
+        compiler_params=params(0),
+    )(flat)
+    return out.reshape(count, rows, cols)
+
+
+def gather_blocks(chunks, n_dp, n_chip, count):
+    _, chunk, cols = chunks.shape
+    piece = chunk // n_chip
+    vmem = pl.BlockSpec(memory_space=pltpu.VMEM)
+    return pl.pallas_call(
+        functools.partial(weight_kernel, n_dp, n_chip),
+        out_shape=jax.ShapeDtypeStruct((2 * n_dp * chunk, cols), chunks.dtype),
+        in_specs=[vmem],
+        out_specs=vmem,
+        scratch_shapes=[
+            pltpu.VMEM((2, chunk, cols), chunks.dtype),
+            pltpu.VMEM((chunk, cols), chunks.dtype),
+            pltpu.VMEM((n_chip, piece, cols), chunks.dtype),
+            pltpu.SemaphoreType.DMA((5, n_chip)),
+            pltpu.SemaphoreType.DMA((5, n_chip)),
+        ],
+        compiler_params=params(1),
+    )(chunks)
+
+
 def body(
     partials,
     owners,
@@ -73,16 +254,17 @@
     basis_right,
 ):
     owner_count = lax.axis_size("owner")
+    n_dp = lax.axis_size("dp")
+    n_chip = owner_count // 2
     slot_count = master.shape[0]
     total_slot_count = slot_count * owner_count
     target, source, occupied = slot_layout(owners, slot_count, total_slot_count)
     first_slot = lax.axis_index("owner") * slot_count
     occupied_mine = lax.dynamic_slice_in_dim(occupied, first_slot, slot_count, 0)
-    own_part = partials[0]
-    mask_all = (occupied > 0).astype(jnp.float32)[:, None, None]
-    placed = jnp.take(own_part, source, axis=0).astype(jnp.float32) * mask_all
-    summed = lax.psum_scatter(placed.astype(jnp.bfloat16), "owner", scatter_dimension=0, tiled=True)
-    gradient = lax.psum(summed, "dp").astype(jnp.float32)
+    source_mine = lax.dynamic_slice_in_dim(source, first_slot, slot_count, 0)
+    grad_sum = all_reduce_blocks(partials[0], n_dp, n_chip)
+    mask_mine = (occupied_mine > 0).astype(jnp.float32)[:, None, None]
+    gradient = jnp.take(grad_sum, source_mine, axis=0).astype(jnp.float32) * mask_mine
     direction, left_new, right_new = soap_update(
         gradient,
         occupied_mine,
@@ -95,8 +277,18 @@
         step_count,
     )
     updated = (master - 0.01 * (direction + 0.1 * master)).astype(jnp.bfloat16)
-    every_slot = lax.all_gather(updated, "owner", axis=0, tiled=True)
-    weights_all = jnp.take(every_slot, target, axis=0)
+    block_count = owners.shape[0]
+    count, rows, cols = block_count, updated.shape[1], updated.shape[2]
+    per = count // (2 * n_dp)
+    rank = target - first_slot
+    in_mine = (rank >= 0) & (rank < slot_count)
+    dense = jnp.where(
+        in_mine[:, None, None], jnp.take(updated, jnp.clip(rank, 0, slot_count - 1), axis=0), 0
+    ).astype(jnp.bfloat16)
+    replica = lax.axis_index("dp")
+    chunks = dense.reshape(2, n_dp, per * rows, cols)
+    chunks = lax.dynamic_index_in_dim(chunks, replica, axis=1, keepdims=False)
+    weights_all = gather_blocks(chunks, n_dp, n_chip, count).reshape(count, rows, cols)
     return (weights_all, direction, left_new, right_new)
 
 

time: 321 us -> 175 us (0.55)
  waiting for transfers between devices: 223 us -> 0 us
  Pallas kernels: 0 us -> 120 us
  local copies, waits for them, and re-layouts: 35.4 us -> 18.2 us
  between operations: 14.7 us -> 1.76 us
  other arithmetic: 13.3 us -> 3.83 us
    pallas_call x0 -> x2, Pallas kernels: none -> 120 us  [the longest x1 75.3 us: all_reduce_blocks(): pl.pallas_call(functools.partial(grad_kernel, n_dp, n_chip), out_shape=ja...]
    reduce_scatter x1 -> x0, waiting for transfers between devices: 112 us -> none  [body(): lax.psum_scatter(placed.astype(jnp.bfloat16), 'owner', scatter_dimension=...]
    psum x1 -> x0, waiting for transfers between devices: 67.6 us -> none  [body(): gradient = lax.psum(summed, 'dp').astype(jnp.float32)]
    all_gather x1 -> x0, waiting for transfers between devices: 43.3 us -> none  [body(): every_slot = lax.all_gather(updated, 'owner', axis=0, tiled=True)]
    gather x3 -> x4, local copies, waits for them, and re-layouts: 22.1 us -> 6.34 us  [the longest x2 3.93 us: body(): jnp.take(updated, jnp.clip(rank, 0, slot_count - 1), axis=0)]
    convert_element_type x2 -> x0, other arithmetic: 7.47 us -> none  [the longest x1 7.46 us: body(): placed.astype(jnp.bfloat16)]
    select_n x3 -> x0, other arithmetic: 3.91 us -> none  [the longest x2 3.91 us: body(): weights_all = jnp.take(every_slot, target, axis=0)]
    unnamed x16 -> x31, local copies, waits for them, and re-layouts: 11.5 us -> 11.2 us
  transfers between devices with their start and end apart: 3 -> 0, of which waited for: 3 -> 0; matrix products, arithmetic and copies ran while one was open for 11% -> 0% of each run, Pallas kernels for 0% -> 0%
where the time goes in v3:
time: 175 us
  Pallas kernels  120 us (69%)
  matrix products  30.8 us (18%)
  local copies, waits for them, and re-layouts  18.2 us (10%)
  other arithmetic  3.83 us (2%)
  between operations  1.76 us (1%)
    pallas_call x1, Pallas kernels, all_reduce_blocks(): pl.pallas_call(functools.partial(grad_kernel, n_dp, n_chip), out_shape=ja...  75.3 us
    pallas_call x1, Pallas kernels, gather_blocks(): pl.pallas_call(functools.partial(weight_kernel, n_dp, n_chip), out_shape=...  44.9 us
    dot_general x34, matrix products, product(): return jnp.matmul(left, right, precision=lax.Precision.HIGHEST)  30.8 us
    unnamed x31, local copies, waits for them, and re-layouts  11.2 us
    gather x2, local copies, waits for them, and re-layouts, body(): jnp.take(updated, jnp.clip(rank, 0, slot_count - 1), axis=0)  3.93 us

profile of v3, /device:TPU:1, one launch (start us, length us, event | category | flops | bytes accessed | tf_op | source)
XLA Modules:
  0.0 174.8 jit_solution(18000543279061946550)
XLA Ops:
  0.6 1.9 %copy.50 = f32[6,128,128]{1,2,0:T(8,128)} copy(f32[6,128,128]{2,1,0:T(8,128)} %param.13) | data formatting | bytes 786432 | tf_op args[3]
  2.5 0.9 convert_reduce_fusion.1
  3.5 1.2 compare_and_fusion.1
  5.4 75.3 %shard_map.129 = bf16[12288,128]{1,0:T(8,128)(2,1)S(1)} custom-call(bf16[12288,128]{1,0:T(8,128)(2,1)} %bitcast.90), custom_call_target="tpu_custom_call" | custom-call | tf_op jit(solution)/shard_map/pallas_call | solution.py:205
  80.7 1.3 gather_fusion
  82.0 1.2 copy.41
  84.0 1.2 copy.44
  85.9 1.7 fusion.22
  89.8 1.7 subtract_convert_fusion
  91.5 1.2 gather_fusion.1
  92.7 2.8 %copy.51 = bf16[96,128,128]{2,1,0:T(8,128)(2,1)} copy(bf16[96,128,128]{1,2,0:T(8,128)(2,1)S(1)} %gather_fusion.1) | data formatting | bytes 6291456 | tf_op jit(solution)/shard_map/jit(_take)/gather | solution.py:286
  96.1 1.5 fusion.24.x_ref
  97.6 44.9 %shard_map.130 = bf16[12288,128]{1,0:T(8,128)(2,1)S(1)} custom-call(bf16[2,768,128]{2,1,0:T(8,128)(2,1)S(1)} %fusion.24.x_ref), custom_call_target="tpu_custom_call" | custom-call | tf_op jit(solution)/shard_map/pallas_call | solution.py:228
  142.5 1.9 %copy.73 = f32[6,128,128]{2,1,0:T(8,128)} copy(f32[6,128,128]{1,2,0:T(8,128)} %get-tuple-element.26) | data formatting | bytes 786432
  144.4 1.9 %copy.52 = f32[6,128,128]{1,2,0:T(8,128)} copy(f32[6,128,128]{2,1,0:T(8,128)} %param.16) | data formatting | bytes 786432 | tf_op args[6]
  146.3 2.1 %fusion.16 = f32[6,128,128]{1,2,0:T(8,128)S(1)} fusion(f32[6,128,128]{1,2,0:T(8,128)} %copy.52, f32[6]{0:T(128)S(1)} %get-tuple-element.31, bf16[6,128,128]{1,2,0:T(8,128)(2,1)} %copy-done.5, pred[6]{0:T(512)(128)(4,1)S(1)} %get-tuple-element.21), kind=kOutput, calls=%fused_computation.34 | convolution fusion | flops 151584768 | bytes 983070 | tf_op jit(solution)/shard_map/dot_general | solution.py:16
  148.4 0.9 multiply_reduce_fusion.1
  149.4 0.9 fusion.36
  157.3 1.3 fusion.10
  158.6 1.9 %copy.63 = f32[6,128,128]{1,2,0:T(8,128)} copy(f32[6,128,128]{2,1,0:T(8,128)} %param.17) | data formatting | bytes 786432 | tf_op args[7]
  160.5 2.3 %fusion.8 = f32[6,128,128]{1,2,0:T(8,128)S(1)} fusion(f32[6,128,128]{1,2,0:T(8,128)} %copy.63, f32[6]{0:T(128)S(1)} %get-tuple-element.31, bf16[6,128,128]{1,2,0:T(8,128)(2,1)} %copy-done.5, pred[6]{0:T(512)(128)(4,1)S(1)} %get-tuple-element.21), kind=kOutput, calls=%fused_computation.19 | convolution fusion | flops 151584768 | bytes 983070 | tf_op jit(solution)/shard_map/dot_general | solution.py:16
  162.8 1.1 multiply_reduce_fusion
  171.8 1.3 fusion.2
  173.1 1.7 copy.101
  (64 shorter events, 19.0 us)
Async XLA Ops:
  4.6 0.5 copy-start.8
  5.4 77.8 %copy-start = (f32[6,128,128]{2,1,0:T(8,128)S(1)}, f32[6,128,128]{2,1,0:T(8,128)}, u32[]{:S(2)}) copy-start(f32[6,128,128]{2,1,0:T(8,128)} %param.19) | copy-start | bytes 1179652
  82.0 5.6 %copy-start.7 = (f32[6,128,128]{2,1,0:T(8,128)S(1)}, f32[6,128,128]{2,1,0:T(8,128)}, u32[]{:S(2)}) copy-start(f32[6,128,128]{2,1,0:T(8,128)} %param.14) | copy-start | bytes 1179652
  82.0 6.7 %copy-start.2 = (f32[6,128,128]{2,1,0:T(8,128)S(1)}, f32[6,128,128]{2,1,0:T(8,128)}, u32[]{:S(2)}) copy-start(f32[6,128,128]{2,1,0:T(8,128)} %param.18) | copy-start | bytes 1179652
  83.1 6.1 %copy-start.5 = (bf16[6,128,128]{1,2,0:T(8,128)(2,1)}, bf16[6,128,128]{1,2,0:T(8,128)(2,1)S(1)}, u32[]{:S(2)}) copy-start(bf16[6,128,128]{1,2,0:T(8,128)(2,1)S(1)} %copy.41) | copy-start | bytes 589828
  85.9 3.9 %copy-start.6 = (f32[6,128,128]{1,2,0:T(8,128)S(1)}, f32[6,128,128]{1,2,0:T(8,128)}, u32[]{:S(2)}) copy-start(f32[6,128,128]{1,2,0:T(8,128)} %copy.50) | copy-start | bytes 1179652
  87.8 3.7 %copy-start.11 = (s32[96]{0:T(128)S(1)}, s32[96]{0:T(128)}, u32[]{:S(2)}) copy-start(s32[96]{0:T(128)} %get-tuple-element.19) | copy-start | bytes 1156
  92.6 2.8 %copy-start.10 = (pred[96]{0:T(512)(128)(4,1)S(1)}, pred[96]{0:T(512)(128)(4,1)}, u32[]{:S(2)}) copy-start(pred[96]{0:T(512)(128)(4,1)} %get-tuple-element.18) | copy-start | bytes 292
  92.7 3.1 %copy-start.9 = (s32[96]{0:T(128)S(1)}, s32[96]{0:T(128)}, u32[]{:S(2)}) copy-start(s32[96]{0:T(128)} %copy-done.8) | copy-start | bytes 1156
  97.6 50.8 %copy-start.3 = (f32[6,128,128]{2,1,0:T(8,128)S(1)}, f32[6,128,128]{2,1,0:T(8,128)}, u32[]{:S(2)}) copy-start(f32[6,128,128]{2,1,0:T(8,128)} %param.18) | copy-start | bytes 1179652
  153.6 3.6 %copy-start.4 = (f32[6,128,128]{2,1,0:T(8,128)S(1)}, f32[6,128,128]{2,1,0:T(8,128)}, u32[]{:S(2)}) copy-start(f32[6,128,128]{2,1,0:T(8,128)} %param.18) | copy-start | bytes 1179652
  155.9 6.9 %copy-start.1 = (f32[6,128,128]{2,1,0:T(8,128)S(1)}, f32[6,128,128]{2,1,0:T(8,128)}, u32[]{:S(2)}) copy-start(f32[6,128,128]{2,1,0:T(8,128)} %param.19) | copy-start | bytes 1179652

commit v4 on v3

--- a/solution.py
+++ b/solution.py
@@ -241,6 +241,60 @@
     )(chunks)
 
 
+def mm(left, right):
+    return jnp.dot(left, right, precision=lax.Precision.HIGHEST, preferred_element_type=jnp.float32)
+
+
+def refresh_one(stat, basis):
+    power = mm(stat, basis)
+    magnitude = jnp.sqrt(jnp.sum(power * power, keepdims=True))
+    iterate = power / (magnitude + 1e-06)
+    for repeat_count in range(NS_ITERS):
+        iterate = 1.5 * iterate - 0.5 * mm(iterate, mm(iterate.T, iterate))
+    return iterate
+
+
+def soap_kernel(
+    scalars, g_ref, m_ref, s_ref, sl_ref, sr_ref, bl_ref, br_ref, w_ref,
+    d_out, l_out, r_out, u_out,
+):
+    slot = pl.program_id(0)
+    correction = scalars[0]
+    occupied = scalars[1 + slot] > 0
+    gradient = g_ref[0]
+    basis_left = bl_ref[0]
+    basis_right = br_ref[0]
+    moment_new = 0.95 * m_ref[0] + 0.05 * gradient
+    rotated = mm(basis_left.T, mm(gradient, basis_right))
+    rot_moment = mm(basis_left.T, mm(moment_new, basis_right))
+    second_new = 0.95 * s_ref[0] + 0.05 * rotated * rotated
+    scaled = rot_moment / correction / (jnp.sqrt(second_new / correction) + 1e-08)
+    direction = jnp.where(occupied, mm(basis_left, mm(scaled, basis_right.T)), 0.0)
+    d_out[0] = direction
+    master = w_ref[0]
+    u_out[0] = (master - 0.01 * (direction + 0.1 * master)).astype(u_out.dtype)
+    left_stat = 0.95 * sl_ref[0] + 0.05 * mm(gradient, gradient.T)
+    right_stat = 0.95 * sr_ref[0] + 0.05 * mm(gradient.T, gradient)
+    l_out[0] = jnp.where(occupied, refresh_one(left_stat, basis_left), basis_left)
+    r_out[0] = jnp.where(occupied, refresh_one(right_stat, basis_right), basis_right)
+
+
+def soap_slots(gradient, occupied, moment, second, stat_left, stat_right, basis_left, basis_right, master, step_count):
+    slots, rows, cols = gradient.shape
+    elapsed = step_count[0].astype(jnp.float32)
+    correction = 1.0 - jnp.power(jnp.float32(0.95), elapsed)
+    scalars = jnp.concatenate([correction[None], occupied.astype(jnp.float32)])
+    block = pl.BlockSpec((1, rows, cols), lambda i: (i, 0, 0))
+    f32 = jax.ShapeDtypeStruct(gradient.shape, jnp.float32)
+    return pl.pallas_call(
+        soap_kernel,
+        grid=(slots,),
+        out_shape=(f32, f32, f32, jax.ShapeDtypeStruct(gradient.shape, jnp.bfloat16)),
+        in_specs=[pl.BlockSpec(memory_space=pltpu.SMEM)] + [block] * 8,
+        out_specs=(block, block, block, block),
+    )(scalars, gradient, moment, second, stat_left, stat_right, basis_left, basis_right, master)
+
+
 def body(
     partials,
     owners,
@@ -265,18 +319,9 @@
     grad_sum = all_reduce_blocks(partials[0], n_dp, n_chip)
     mask_mine = (occupied_mine > 0).astype(jnp.float32)[:, None, None]
     gradient = jnp.take(grad_sum, source_mine, axis=0).astype(jnp.float32) * mask_mine
-    direction, left_new, right_new = soap_update(
-        gradient,
-        occupied_mine,
-        moment,
-        second,
-        stat_left,
-        stat_right,
-        basis_left,
-        basis_right,
-        step_count,
-    )
-    updated = (master - 0.01 * (direction + 0.1 * master)).astype(jnp.bfloat16)
+    direction, left_new, right_new, updated = soap_slots(
+        gradient, occupied_mine, moment, second, stat_left, stat_right, basis_left, basis_right, master, step_count
+    )
     block_count = owners.shape[0]
     count, rows, cols = block_count, updated.shape[1], updated.shape[2]
     per = count // (2 * n_dp)

time: 175 us -> 178 us (1.017)
  Pallas kernels: 120 us -> 168 us
  matrix products: 30.8 us -> 0 us
  local copies, waits for them, and re-layouts: 18.2 us -> 4.95 us
    pallas_call x0 -> x1, Pallas kernels: none -> 47.6 us  [soap_slots(): pl.pallas_call(soap_kernel, grid=(slots,), out_shape=(f32, f32, f32, jax....]
    dot_general x34 -> x0, matrix products: 30.8 us -> none  [product(): return jnp.matmul(left, right, precision=lax.Precision.HIGHEST)]
    unnamed x31 -> x1, local copies, waits for them, and re-layouts: 11.2 us -> 1.67 us
    gather x2 -> x1, local copies, waits for them, and re-layouts: 3.93 us -> 2.08 us  [body(): jnp.take(updated, jnp.clip(rank, 0, slot_count - 1), axis=0)]
    gather x2 -> x1, local copies, waits for them, and re-layouts: 2.41 us -> 0.58 us  [body(): jnp.take(grad_sum, source_mine, axis=0).astype(jnp.float32) * mask_mine]
where the time goes in v4:
time: 178 us
  Pallas kernels  168 us (94%)
  local copies, waits for them, and re-layouts  4.95 us (3%)
  other arithmetic  3.98 us (2%)
    pallas_call x1, Pallas kernels, all_reduce_blocks(): pl.pallas_call(functools.partial(grad_kernel, n_dp, n_chip), out_shape=ja...  75.4 us
    pallas_call x1, Pallas kernels, soap_slots(): pl.pallas_call(soap_kernel, grid=(slots,), out_shape=(f32, f32, f32, jax....  47.6 us
    pallas_call x1, Pallas kernels, gather_blocks(): pl.pallas_call(functools.partial(weight_kernel, n_dp, n_chip), out_shape=...  44.7 us

profile of v4, /device:TPU:1, one launch (start us, length us, event | category | flops | bytes accessed | tf_op | source)
XLA Modules:
  0.0 178.0 jit_solution(201853616476638513)
XLA Ops:
  1.3 0.9 convert_reduce_fusion.1
  2.2 0.7 compare_and_fusion.1
  2.9 0.1 broadcast_in_dim.62
  3.0 0.1 copy.24
  3.1 0.1 broadcast_in_dim.58
  3.2 0.1 copy.22
  3.3 0.1 select_reduce_fusion
  3.4 0.1 dynamic-slice_convert_fusion
  3.5 0.1 compare_and_fusion
  3.6 0.7 pad_maximum_fusion.scalars
  4.3 0.1 broadcast_bitcast_fusion.1
  4.3 0.1 broadcast_bitcast_fusion
  4.5 75.4 %shard_map.129 = bf16[12288,128]{1,0:T(8,128)(2,1)S(1)} custom-call(bf16[12288,128]{1,0:T(8,128)(2,1)} %bitcast.13), custom_call_target="tpu_custom_call" | custom-call | tf_op jit(solution)/shard_map/pallas_call | solution.py:205
  79.9 0.6 gather_fusion
  80.5 0.9 convert_multiply_fusion.g_ref
  81.4 47.6 %shard_map.130 = (f32[6,128,128]{2,1,0:T(8,128)}, f32[6,128,128]{2,1,0:T(8,128)}, f32[6,128,128]{2,1,0:T(8,128)}, bf16[6,128,128]{2,1,0:T(8,128)(2,1)}) custom-call(f32[7]{0:T(128)} %pad_maximum_fusion.scalars, f32[6,128,128]{2,1,0:T(8,128)} %convert_multiply_fusion.g_ref, f32[6,128,128]{2,1,0:T(8,128)} %m_ref.1, f32[6,128,128]{2,1,0:T(8,128)} %s_ref.1, ...), custom_call_target="tpu_custom_call" | custom-call | tf_op jit(solution)/shard_map/pallas_call | solution.py:289
  129.0 2.1 %gather_fusion.1 = bf16[96,128,128]{2,1,0:T(8,128)(2,1)S(1)} fusion(bf16[6,128,128]{2,1,0:T(8,128)(2,1)} %get-tuple-element.8, s32[1024]{0:T(1024)S(1)} %pad_clamp_fusion), kind=kCustom, calls=%fused_computation.1 | custom fusion | bytes 6291840 | tf_op jit(solution)/shard_map/jit(_take)/gather | solution.py:331
  131.0 0.6 fusion.1.x_ref
  131.6 44.7 %shard_map.131 = bf16[12288,128]{1,0:T(8,128)(2,1)S(1)} custom-call(bf16[2,768,128]{2,1,0:T(8,128)(2,1)S(1)} %fusion.1.x_ref), custom_call_target="tpu_custom_call" | custom-call | tf_op jit(solution)/shard_map/pallas_call | solution.py:228
  176.3 1.7 copy.35
  (6 shorter events, 0.1 us)

commit v5 on v3

--- a/solution.py
+++ b/solution.py
@@ -241,6 +241,64 @@
     )(chunks)
 
 
+def split(a):
+    hi = a.astype(jnp.bfloat16)
+    lo = (a - hi.astype(jnp.float32)).astype(jnp.bfloat16)
+    return hi, lo
+
+def mm3(left, right):
+    lh, ll = split(left)
+    rh, rl = split(right)
+    dot = functools.partial(jnp.dot, preferred_element_type=jnp.float32)
+    return dot(lh, rh) + (dot(lh, rl) + dot(ll, rh))
+
+def soap_kernel(scalars, g_ref, m_ref, s_ref, sl_ref, sr_ref, bl_ref, br_ref, w_ref, d_out, l_out, r_out, u_out):
+    slots = g_ref.shape[0]
+    correction = scalars[0]
+    chains = []
+    for i in range(slots):
+        occupied = scalars[1 + i] > 0
+        gradient = g_ref[i]
+        basis_left = bl_ref[i]
+        basis_right = br_ref[i]
+        moment_new = 0.95 * m_ref[i] + 0.05 * gradient
+        rotated = mm3(basis_left.T, mm3(gradient, basis_right))
+        rot_moment = mm3(basis_left.T, mm3(moment_new, basis_right))
+        second_new = 0.95 * s_ref[i] + 0.05 * rotated * rotated
+        scaled = rot_moment / correction / (jnp.sqrt(second_new / correction) + 1e-08)
+        direction = jnp.where(occupied, mm3(basis_left, mm3(scaled, basis_right.T)), 0.0)
+        d_out[i] = direction
+        master = w_ref[i]
+        u_out[i] = (master - 0.01 * (direction + 0.1 * master)).astype(u_out.dtype)
+        left_stat = 0.95 * sl_ref[i] + 0.05 * mm3(gradient, gradient.T)
+        right_stat = 0.95 * sr_ref[i] + 0.05 * mm3(gradient.T, gradient)
+        chains.append((left_stat, basis_left, l_out, i, occupied))
+        chains.append((right_stat, basis_right, r_out, i, occupied))
+    iterates = []
+    for stat, basis, out, i, occupied in chains:
+        power = mm3(stat, basis)
+        magnitude = jnp.sqrt(jnp.sum(power * power, keepdims=True))
+        iterates.append(power / (magnitude + 1e-06))
+    for repeat_count in range(NS_ITERS):
+        grams = [mm3(it.T, it) for it in iterates]
+        iterates = [1.5 * it - 0.5 * mm3(it, gram) for it, gram in zip(iterates, grams)]
+    for (stat, basis, out, i, occupied), it in zip(chains, iterates):
+        out[i] = jnp.where(occupied, it, basis)
+
+def soap_slots(gradient, occupied, moment, second, stat_left, stat_right, basis_left, basis_right, master, step_count):
+    elapsed = step_count[0].astype(jnp.float32)
+    correction = 1.0 - jnp.power(jnp.float32(0.95), elapsed)
+    scalars = jnp.concatenate([correction[None], occupied.astype(jnp.float32)])
+    vmem = pl.BlockSpec(memory_space=pltpu.VMEM)
+    f32 = jax.ShapeDtypeStruct(gradient.shape, jnp.float32)
+    return pl.pallas_call(
+        soap_kernel,
+        out_shape=(f32, f32, f32, jax.ShapeDtypeStruct(gradient.shape, jnp.bfloat16)),
+        in_specs=[pl.BlockSpec(memory_space=pltpu.SMEM)] + [vmem] * 8,
+        out_specs=(vmem, vmem, vmem, vmem),
+    )(scalars, gradient, moment, second, stat_left, stat_right, basis_left, basis_right, master)
+
+
 def body(
     partials,
     owners,
@@ -265,18 +323,9 @@
     grad_sum = all_reduce_blocks(partials[0], n_dp, n_chip)
     mask_mine = (occupied_mine > 0).astype(jnp.float32)[:, None, None]
     gradient = jnp.take(grad_sum, source_mine, axis=0).astype(jnp.float32) * mask_mine
-    direction, left_new, right_new = soap_update(
-        gradient,
-        occupied_mine,
-        moment,
-        second,
-        stat_left,
-        stat_right,
-        basis_left,
-        basis_right,
-        step_count,
-    )
-    updated = (master - 0.01 * (direction + 0.1 * master)).astype(jnp.bfloat16)
+    direction, left_new, right_new, updated = soap_slots(
+        gradient, occupied_mine, moment, second, stat_left, stat_right, basis_left, basis_right, master, step_count
+    )
     block_count = owners.shape[0]
     count, rows, cols = block_count, updated.shape[1], updated.shape[2]
     per = count // (2 * n_dp)

time: 175 us -> 141 us (0.81)
  matrix products: 30.8 us -> 0 us
  local copies, waits for them, and re-layouts: 18.2 us -> 4.95 us
  Pallas kernels: 120 us -> 130 us
    dot_general x34 -> x0, matrix products: 30.8 us -> none  [product(): return jnp.matmul(left, right, precision=lax.Precision.HIGHEST)]
    pallas_call x0 -> x1, Pallas kernels: none -> 10.2 us  [soap_slots(): pl.pallas_call(soap_kernel, out_shape=(f32, f32, f32, jax.ShapeDtypeStruc...]
    unnamed x31 -> x1, local copies, waits for them, and re-layouts: 11.2 us -> 1.67 us
    gather x2 -> x1, local copies, waits for them, and re-layouts: 3.93 us -> 2.08 us  [body(): jnp.take(updated, jnp.clip(rank, 0, slot_count - 1), axis=0)]
    gather x2 -> x1, local copies, waits for them, and re-layouts: 2.41 us -> 0.58 us  [body(): jnp.take(grad_sum, source_mine, axis=0).astype(jnp.float32) * mask_mine]
where the time goes in v5:
time: 141 us
  Pallas kernels  130 us (92%)
  local copies, waits for them, and re-layouts  4.95 us (4%)
  other arithmetic  3.98 us (3%)
  between operations  1.43 us (1%)
    pallas_call x1, Pallas kernels, all_reduce_blocks(): pl.pallas_call(functools.partial(grad_kernel, n_dp, n_chip), out_shape=ja...  75.4 us
    pallas_call x1, Pallas kernels, gather_blocks(): pl.pallas_call(functools.partial(weight_kernel, n_dp, n_chip), out_shape=...  44.7 us
    pallas_call x1, Pallas kernels, soap_slots(): pl.pallas_call(soap_kernel, out_shape=(f32, f32, f32, jax.ShapeDtypeStruc...  10.2 us

profile of v5, /device:TPU:1, one launch (start us, length us, event | category | flops | bytes accessed | tf_op | source)
XLA Modules:
  0.0 140.6 jit_solution(6555974768440191966)
XLA Ops:
  1.3 0.9 convert_reduce_fusion.1
  2.2 0.7 compare_and_fusion.1
  2.9 0.1 broadcast_in_dim.62
  3.0 0.1 copy.24
  3.1 0.1 broadcast_in_dim.58
  3.2 0.1 copy.22
  3.3 0.1 select_reduce_fusion
  3.4 0.1 dynamic-slice_convert_fusion
  3.5 0.1 compare_and_fusion
  3.6 0.7 pad_maximum_fusion.scalars
  4.3 0.1 broadcast_bitcast_fusion.1
  4.3 0.1 broadcast_bitcast_fusion
  4.5 75.4 %shard_map.129 = bf16[12288,128]{1,0:T(8,128)(2,1)S(1)} custom-call(bf16[12288,128]{1,0:T(8,128)(2,1)} %bitcast.13), custom_call_target="tpu_custom_call" | custom-call | tf_op jit(solution)/shard_map/pallas_call | solution.py:205
  79.9 0.6 gather_fusion
  80.5 0.9 convert_multiply_fusion.g_ref
  81.4 10.2 %shard_map.130 = (f32[6,128,128]{2,1,0:T(8,128)}, f32[6,128,128]{2,1,0:T(8,128)}, f32[6,128,128]{2,1,0:T(8,128)}, bf16[6,128,128]{2,1,0:T(8,128)(2,1)}) custom-call(f32[7]{0:T(128)} %pad_maximum_fusion.scalars, f32[6,128,128]{2,1,0:T(8,128)} %convert_multiply_fusion.g_ref, f32[6,128,128]{2,1,0:T(8,128)} %m_ref.1, f32[6,128,128]{2,1,0:T(8,128)} %s_ref.1, ...), custom_call_target="tpu_custom_call" | custom-call | tf_op jit(solution)/shard_map/pallas_call | solution.py:294
  91.6 2.1 %gather_fusion.1 = bf16[96,128,128]{2,1,0:T(8,128)(2,1)S(1)} fusion(bf16[6,128,128]{2,1,0:T(8,128)(2,1)} %get-tuple-element.8, s32[1024]{0:T(1024)S(1)} %pad_clamp_fusion), kind=kCustom, calls=%fused_computation.1 | custom fusion | bytes 6291840 | tf_op jit(solution)/shard_map/jit(_take)/gather | solution.py:335
  93.6 0.6 fusion.1.x_ref
  94.2 44.7 %shard_map.131 = bf16[12288,128]{1,0:T(8,128)(2,1)S(1)} custom-call(bf16[2,768,128]{2,1,0:T(8,128)(2,1)S(1)} %fusion.1.x_ref), custom_call_target="tpu_custom_call" | custom-call | tf_op jit(solution)/shard_map/pallas_call | solution.py:228
  138.9 1.7 %copy.35 = bf16[96,128,128]{2,1,0:T(8,128)(2,1)} copy(bf16[96,128,128]{2,1,0:T(8,128)(2,1)S(1)} %bitcast.10) | data formatting | bytes 6291456
  (6 shorter events, 0.1 us)

commit v6 on v5

--- a/solution.py
+++ b/solution.py
@@ -154,12 +154,13 @@
     return (2, core_me, core_peer), (n_dp, dp_me, dp_peer), (n_chip, chip_me, chip_peer)
 
 
-def grad_kernel(n_dp, n_chip, p_ref, o_ref, buf1, hbuf, buf2, mbuf, buf3, send, recv):
+def grad_kernel(n_dp, n_chip, sel, p_ref, o_ref, buf1, hbuf, buf2, mbuf, buf3, held, cube, stage, got, send, recv):
     core, dp, chip = groups_of(n_dp, n_chip)
     enter((core, dp, chip))
     half = p_ref.shape[0] // 2
     chunk = half // n_dp
     piece = chunk // n_chip
+    rows = o_ref.shape[0] // sel.shape[1]
     c, r, m = core[1], dp[1], chip[1]
     finish(phase(core, lambda j: p_ref.at[pl.ds(j * half, half)], lambda me: buf1.at[1], send.at[0], recv.at[0]))
     buf1[0] = p_ref[pl.ds(c * half, half), :]
@@ -169,8 +170,26 @@
     sum_slots(buf2, mbuf, n_dp, chunk, 0)
     buf3[m] = mbuf[pl.ds(m * piece, piece), :]
     finish(phase(chip, lambda j: mbuf.at[pl.ds(j * piece, piece)], lambda me: buf3.at[me], send.at[2], recv.at[2]))
-    sum_slots(buf3, o_ref, n_chip, piece, c * half + r * chunk + m * piece)
-    spread_phases(o_ref, core, dp, chip, piece, send, recv, 3)
+    sum_slots(buf3, held, n_chip, piece, r * chunk + m * piece)
+    finish(phase(chip, lambda j: held.at[pl.ds(r * chunk + m * piece, piece)],
+                 lambda me: held.at[pl.ds(r * chunk + me * piece, piece)], send.at[3], recv.at[3]))
+    finish(phase(dp, lambda j: held.at[pl.ds(r * chunk, chunk)],
+                 lambda me: held.at[pl.ds(me * chunk, chunk)], send.at[4], recv.at[4]))
+    blocks = half // rows
+
+    def to_blocks(i, carry):
+        cube[i] = held[pl.ds(pl.multiple_of(i * rows, rows), rows), :]
+        return carry
+
+    lax.fori_loop(0, blocks, to_blocks, 0)
+    for who, out in ((1, stage), (0, o_ref)):
+        for k in range(sel.shape[1]):
+            block = sel[who, k] - c * blocks
+            inside = (block >= 0) & (block < blocks)
+            value = cube[jnp.clip(block, 0, blocks - 1)]
+            out[pl.ds(k * rows, rows), :] = jnp.where(inside, value, jnp.zeros_like(value))
+    finish(phase(core, lambda j: stage, lambda me: got, send.at[5], recv.at[5]))
+    o_ref[...] = o_ref[...] + got[...]
 
 
 def weight_kernel(n_dp, n_chip, x_ref, o_ref, buf1, pbuf, buf3, send, recv):
@@ -195,8 +214,9 @@
     )
 
 
-def all_reduce_blocks(blocks, n_dp, n_chip):
+def owned_gradient(blocks, sel, n_dp, n_chip):
     count, rows, cols = blocks.shape
+    slots = sel.shape[1]
     flat = blocks.reshape(count * rows, cols)
     half = count * rows // 2
     chunk = half // n_dp
@@ -204,8 +224,8 @@
     vmem = pl.BlockSpec(memory_space=pltpu.VMEM)
     out = pl.pallas_call(
         functools.partial(grad_kernel, n_dp, n_chip),
-        out_shape=jax.ShapeDtypeStruct(flat.shape, flat.dtype),
-        in_specs=[vmem],
+        out_shape=jax.ShapeDtypeStruct((slots * rows, cols), flat.dtype),
+        in_specs=[pl.BlockSpec(memory_space=pltpu.SMEM), vmem],
         out_specs=vmem,
         scratch_shapes=[
             pltpu.VMEM((2, half, cols), flat.dtype),
@@ -213,12 +233,16 @@
             pltpu.VMEM((n_dp, chunk, cols), flat.dtype),
             pltpu.VMEM((chunk, cols), flat.dtype),
             pltpu.VMEM((n_chip, piece, cols), flat.dtype),
+            pltpu.VMEM((half, cols), flat.dtype),
+            pltpu.VMEM((half // rows, rows, cols), flat.dtype),
+            pltpu.VMEM((slots * rows, cols), flat.dtype),
+            pltpu.VMEM((slots * rows, cols), flat.dtype),
             pltpu.SemaphoreType.DMA((6, n_chip)),
             pltpu.SemaphoreType.DMA((6, n_chip)),
         ],
         compiler_params=params(0),
-    )(flat)
-    return out.reshape(count, rows, cols)
+    )(sel, flat)
+    return out.reshape(slots, rows, cols)
 
 
 def gather_blocks(chunks, n_dp, n_chip, count):
@@ -320,9 +344,11 @@
     first_slot = lax.axis_index("owner") * slot_count
     occupied_mine = lax.dynamic_slice_in_dim(occupied, first_slot, slot_count, 0)
     source_mine = lax.dynamic_slice_in_dim(source, first_slot, slot_count, 0)
-    grad_sum = all_reduce_blocks(partials[0], n_dp, n_chip)
+    partner_slot = (lax.axis_index("owner") ^ 1) * slot_count
+    source_partner = lax.dynamic_slice_in_dim(source, partner_slot, slot_count, 0)
+    sel = jnp.stack([source_mine, source_partner]).astype(jnp.int32)
     mask_mine = (occupied_mine > 0).astype(jnp.float32)[:, None, None]
-    gradient = jnp.take(grad_sum, source_mine, axis=0).astype(jnp.float32) * mask_mine
+    gradient = owned_gradient(partials[0], sel, n_dp, n_chip).astype(jnp.float32) * mask_mine
     direction, left_new, right_new, updated = soap_slots(
         gradient, occupied_mine, moment, second, stat_left, stat_right, basis_left, basis_right, master, step_count
     )

time: 141 us -> 139 us (0.986)
  Pallas kernels: 130 us -> 127 us
    pallas_call x1, Pallas kernels: 75.4 us -> 72.5 us  [owned_gradient(): pl.pallas_call(functools.partial(grad_kernel, n_dp, n_chip), out_shape=ja...]
    unnamed x1 -> x3, local copies, waits for them, and re-layouts: 1.67 us -> 3.55 us
where the time goes in v6:
time: 139 us
  Pallas kernels  127 us (91%)
  local copies, waits for them, and re-layouts  6.33 us (5%)
  other arithmetic  3.95 us (3%)
  between operations  1.43 us (1%)
    pallas_call x1, Pallas kernels, owned_gradient(): pl.pallas_call(functools.partial(grad_kernel, n_dp, n_chip), out_shape=ja...  72.5 us
    pallas_call x1, Pallas kernels, gather_blocks(): pl.pallas_call(functools.partial(weight_kernel, n_dp, n_chip), out_shape=...  44.4 us
    pallas_call x1, Pallas kernels, soap_slots(): pl.pallas_call(soap_kernel, out_shape=(f32, f32, f32, jax.ShapeDtypeStruc...  10.2 us
    unnamed x3, local copies, waits for them, and re-layouts  3.55 us

profile of v6, /device:TPU:1, one launch (start us, length us, event | category | flops | bytes accessed | tf_op | source)
XLA Modules:
  0.0 138.8 jit_solution(4300194231345269089)
XLA Ops:
  1.3 0.9 convert_reduce_fusion.1
  2.2 0.7 compare_and_fusion
  2.9 0.1 broadcast_in_dim.50
  3.0 0.1 copy.24
  3.1 0.1 broadcast_in_dim.46
  3.2 0.1 copy.22
  3.3 0.1 select_reduce_fusion
  3.4 0.1 dynamic-slice_bitcast_fusion.1
  3.5 0.1 compare_convert_fusion
  3.6 0.1 dynamic-slice_convert_fusion
  3.7 0.7 pad_maximum_fusion.scalars
  4.3 0.1 broadcast_bitcast_fusion.1
  4.4 0.1 broadcast_bitcast_fusion
  4.6 0.0 copy-start
  4.6 1.9 %copy-done = bf16[1,96,128,128]{3,2,1,0:T(8,128)(2,1)S(1)} copy-done((bf16[1,96,128,128]{3,2,1,0:T(8,128)(2,1)S(1)}, bf16[1,96,128,128]{3,2,1,0:T(8,128)(2,1)}, u32[]{:S(2)}) %copy-start) | copy-done | bytes 3145752
  6.5 72.5 %shard_map.129 = bf16[768,128]{1,0:T(8,128)(2,1)S(1)} custom-call(s32[2,6]{1,0:T(2,128)S(1)} %pad_add_fusion.sel, bf16[12288,128]{1,0:T(8,128)(2,1)S(1)} %bitcast.16), custom_call_target="tpu_custom_call" | custom-call | tf_op jit(solution)/shard_map/pallas_call | solution.py:225
  79.0 0.8 convert_multiply_fusion.g_ref
  79.8 10.2 %shard_map.130 = (f32[6,128,128]{2,1,0:T(8,128)}, f32[6,128,128]{2,1,0:T(8,128)}, f32[6,128,128]{2,1,0:T(8,128)}, bf16[6,128,128]{2,1,0:T(8,128)(2,1)}) custom-call(f32[7]{0:T(128)} %pad_maximum_fusion.scalars, f32[6,128,128]{2,1,0:T(8,128)} %convert_multiply_fusion.g_ref, f32[6,128,128]{2,1,0:T(8,128)} %m_ref.1, f32[6,128,128]{2,1,0:T(8,128)} %s_ref.1, ...), custom_call_target="tpu_custom_call" | custom-call | tf_op jit(solution)/shard_map/pallas_call | solution.py:318
  90.1 2.1 %gather_fusion = bf16[96,128,128]{2,1,0:T(8,128)(2,1)S(1)} fusion(bf16[6,128,128]{2,1,0:T(8,128)(2,1)} %get-tuple-element.8, s32[1024]{0:T(1024)S(1)} %pad_clamp_fusion), kind=kCustom, calls=%fused_computation | custom fusion | bytes 6291840 | tf_op jit(solution)/shard_map/jit(_take)/gather | solution.py:361
  92.1 0.6 fusion.1.x_ref
  92.7 44.4 %shard_map.131 = bf16[12288,128]{1,0:T(8,128)(2,1)S(1)} custom-call(bf16[2,768,128]{2,1,0:T(8,128)(2,1)S(1)} %fusion.1.x_ref), custom_call_target="tpu_custom_call" | custom-call | tf_op jit(solution)/shard_map/pallas_call | solution.py:252
  137.2 1.7 %copy.35 = bf16[96,128,128]{2,1,0:T(8,128)(2,1)} copy(bf16[96,128,128]{2,1,0:T(8,128)(2,1)S(1)} %bitcast.15) | data formatting | bytes 6291456
  (6 shorter events, 0.1 us)
Async XLA Ops:
  4.6 1.9 %copy-start = (bf16[1,96,128,128]{3,2,1,0:T(8,128)(2,1)S(1)}, bf16[1,96,128,128]{3,2,1,0:T(8,128)(2,1)}, u32[]{:S(2)}) copy-start(bf16[1,96,128,128]{3,2,1,0:T(8,128)(2,1)} %param.10) | copy-start | bytes 9437188

commit v7 on v6

--- a/solution.py
+++ b/solution.py
@@ -133,7 +133,7 @@
     lax.fori_loop(0, rows // step, one, 0)
 
 
-def spread_phases(o_ref, core, dp, chip, piece, send, recv, first):
+def spread_phases(o_ref, core, dp, chip, piece, send, recv, first, during):
     n_dp, n_chip = dp[0], chip[0]
     c, r, m = core[1], dp[1], chip[1]
     chunk = n_chip * piece
@@ -141,8 +141,10 @@
     base = c * half + r * chunk
     finish(phase(chip, lambda j: o_ref.at[pl.ds(base + m * piece, piece)],
                  lambda me: o_ref.at[pl.ds(base + me * piece, piece)], send.at[first], recv.at[first]))
-    finish(phase(dp, lambda j: o_ref.at[pl.ds(c * half + r * chunk, chunk)],
-                 lambda me: o_ref.at[pl.ds(c * half + me * chunk, chunk)], send.at[first + 1], recv.at[first + 1]))
+    copies = phase(dp, lambda j: o_ref.at[pl.ds(c * half + r * chunk, chunk)],
+                   lambda me: o_ref.at[pl.ds(c * half + me * chunk, chunk)], send.at[first + 1], recv.at[first + 1])
+    during()
+    finish(copies)
     finish(phase(core, lambda j: o_ref.at[pl.ds(c * half, half)],
                  lambda me: o_ref.at[pl.ds(me * half, half)], send.at[first + 2], recv.at[first + 2]))
 
@@ -192,7 +194,31 @@
     o_ref[...] = o_ref[...] + got[...]
 
 
-def weight_kernel(n_dp, n_chip, x_ref, o_ref, buf1, pbuf, buf3, send, recv):
+def refresh_slots(scalars, g_ref, sl_ref, sr_ref, bl_ref, br_ref, l_out, r_out):
+    chains = []
+    for i in range(g_ref.shape[0]):
+        occupied = scalars[1 + i] > 0
+        gradient = g_ref[i]
+        left_stat = 0.95 * sl_ref[i] + 0.05 * mm3(gradient, gradient.T)
+        right_stat = 0.95 * sr_ref[i] + 0.05 * mm3(gradient.T, gradient)
+        chains.append((left_stat, bl_ref[i], l_out, i, occupied))
+        chains.append((right_stat, br_ref[i], r_out, i, occupied))
+    iterates = []
+    for stat, basis, out, i, occupied in chains:
+        power = mm3(stat, basis)
+        magnitude = jnp.sqrt(jnp.sum(power * power, keepdims=True))
+        iterates.append(power / (magnitude + 1e-06))
+    for repeat_count in range(NS_ITERS):
+        grams = [mm3(it.T, it) for it in iterates]
+        iterates = [1.5 * it - 0.5 * mm3(it, gram) for it, gram in zip(iterates, grams)]
+    for (stat, basis, out, i, occupied), it in zip(chains, iterates):
+        out[i] = jnp.where(occupied, it, basis)
+
+
+def weight_kernel(
+    n_dp, n_chip, scalars, x_ref, g_ref, sl_ref, sr_ref, bl_ref, br_ref,
+    o_ref, l_out, r_out, buf1, pbuf, buf3, send, recv,
+):
     core, dp, chip = groups_of(n_dp, n_chip)
     enter((core, dp, chip))
     chunk = x_ref.shape[1]
@@ -205,7 +231,11 @@
     buf3[m] = pbuf[pl.ds(m * piece, piece), :]
     finish(phase(chip, lambda j: pbuf.at[pl.ds(j * piece, piece)], lambda me: buf3.at[me], send.at[1], recv.at[1]))
     sum_slots(buf3, o_ref, n_chip, piece, c * half + r * chunk + m * piece)
-    spread_phases(o_ref, core, dp, chip, piece, send, recv, 2)
+
+    def during():
+        refresh_slots(scalars, g_ref, sl_ref, sr_ref, bl_ref, br_ref, l_out, r_out)
+
+    spread_phases(o_ref, core, dp, chip, piece, send, recv, 2, during)
 
 
 def params(collective_id):
@@ -245,15 +275,16 @@
     return out.reshape(slots, rows, cols)
 
 
-def gather_blocks(chunks, n_dp, n_chip, count):
+def gather_blocks(chunks, n_dp, n_chip, scalars, gradient, stat_left, stat_right, basis_left, basis_right):
     _, chunk, cols = chunks.shape
     piece = chunk // n_chip
     vmem = pl.BlockSpec(memory_space=pltpu.VMEM)
+    f32 = jax.ShapeDtypeStruct(gradient.shape, jnp.float32)
     return pl.pallas_call(
         functools.partial(weight_kernel, n_dp, n_chip),
-        out_shape=jax.ShapeDtypeStruct((2 * n_dp * chunk, cols), chunks.dtype),
-        in_specs=[vmem],
-        out_specs=vmem,
+        out_shape=(jax.ShapeDtypeStruct((2 * n_dp * chunk, cols), chunks.dtype), f32, f32),
+        in_specs=[pl.BlockSpec(memory_space=pltpu.SMEM)] + [vmem] * 6,
+        out_specs=(vmem, vmem, vmem),
         scratch_shapes=[
             pltpu.VMEM((2, chunk, cols), chunks.dtype),
             pltpu.VMEM((chunk, cols), chunks.dtype),
@@ -262,7 +293,7 @@
             pltpu.SemaphoreType.DMA((5, n_chip)),
         ],
         compiler_params=params(1),
-    )(chunks)
+    )(scalars, chunks, gradient, stat_left, stat_right, basis_left, basis_right)
 
 
 def split(a):
@@ -276,10 +307,9 @@
     dot = functools.partial(jnp.dot, preferred_element_type=jnp.float32)
     return dot(lh, rh) + (dot(lh, rl) + dot(ll, rh))
 
-def soap_kernel(scalars, g_ref, m_ref, s_ref, sl_ref, sr_ref, bl_ref, br_ref, w_ref, d_out, l_out, r_out, u_out):
+def soap_kernel(scalars, g_ref, m_ref, s_ref, bl_ref, br_ref, w_ref, d_out, u_out):
     slots = g_ref.shape[0]
     correction = scalars[0]
-    chains = []
     for i in range(slots):
         occupied = scalars[1 + i] > 0
         gradient = g_ref[i]
@@ -294,33 +324,23 @@
         d_out[i] = direction
         master = w_ref[i]
         u_out[i] = (master - 0.01 * (direction + 0.1 * master)).astype(u_out.dtype)
-        left_stat = 0.95 * sl_ref[i] + 0.05 * mm3(gradient, gradient.T)
-        right_stat = 0.95 * sr_ref[i] + 0.05 * mm3(gradient.T, gradient)
-        chains.append((left_stat, basis_left, l_out, i, occupied))
-        chains.append((right_stat, basis_right, r_out, i, occupied))
-    iterates = []
-    for stat, basis, out, i, occupied in chains:
-        power = mm3(stat, basis)
-        magnitude = jnp.sqrt(jnp.sum(power * power, keepdims=True))
-        iterates.append(power / (magnitude + 1e-06))
-    for repeat_count in range(NS_ITERS):
-        grams = [mm3(it.T, it) for it in iterates]
-        iterates = [1.5 * it - 0.5 * mm3(it, gram) for it, gram in zip(iterates, grams)]
-    for (stat, basis, out, i, occupied), it in zip(chains, iterates):
-        out[i] = jnp.where(occupied, it, basis)
-
-def soap_slots(gradient, occupied, moment, second, stat_left, stat_right, basis_left, basis_right, master, step_count):
+
+
+def soap_scalars(occupied, step_count):
     elapsed = step_count[0].astype(jnp.float32)
     correction = 1.0 - jnp.power(jnp.float32(0.95), elapsed)
-    scalars = jnp.concatenate([correction[None], occupied.astype(jnp.float32)])
+    return jnp.concatenate([correction[None], occupied.astype(jnp.float32)])
+
+
+def soap_slots(scalars, gradient, moment, second, basis_left, basis_right, master):
     vmem = pl.BlockSpec(memory_space=pltpu.VMEM)
     f32 = jax.ShapeDtypeStruct(gradient.shape, jnp.float32)
     return pl.pallas_call(
         soap_kernel,
-        out_shape=(f32, f32, f32, jax.ShapeDtypeStruct(gradient.shape, jnp.bfloat16)),
-        in_specs=[pl.BlockSpec(memory_space=pltpu.SMEM)] + [vmem] * 8,
-        out_specs=(vmem, vmem, vmem, vmem),
-    )(scalars, gradient, moment, second, stat_left, stat_right, basis_left, basis_right, master)
+        out_shape=(f32, jax.ShapeDtypeStruct(gradient.shape, jnp.bfloat16)),
+        in_specs=[pl.BlockSpec(memory_space=pltpu.SMEM)] + [vmem] * 6,
+        out_specs=(vmem, vmem),
+    )(scalars, gradient, moment, second, basis_left, basis_right, master)
 
 
 def body(
@@ -349,9 +369,8 @@
     sel = jnp.stack([source_mine, source_partner]).astype(jnp.int32)
     mask_mine = (occupied_mine > 0).astype(jnp.float32)[:, None, None]
     gradient = owned_gradient(partials[0], sel, n_dp, n_chip).astype(jnp.float32) * mask_mine
-    direction, left_new, right_new, updated = soap_slots(
-        gradient, occupied_mine, moment, second, stat_left, stat_right, basis_left, basis_right, master, step_count
-    )
+    scalars = soap_scalars(occupied_mine, step_count)
+    direction, updated = soap_slots(scalars, gradient, moment, second, basis_left, basis_right, master)
     block_count = owners.shape[0]
     count, rows, cols = block_count, updated.shape[1], updated.shape[2]
     per = count // (2 * n_dp)
@@ -363,7 +382,10 @@
     replica = lax.axis_index("dp")
     chunks = dense.reshape(2, n_dp, per * rows, cols)
     chunks = lax.dynamic_index_in_dim(chunks, replica, axis=1, keepdims=False)
-    weights_all = gather_blocks(chunks, n_dp, n_chip, count).reshape(count, rows, cols)
+    weights_flat, left_new, right_new = gather_blocks(
+        chunks, n_dp, n_chip, scalars, gradient, stat_left, stat_right, basis_left, basis_right
+    )
+    weights_all = weights_flat.reshape(count, rows, cols)
     return (weights_all, direction, left_new, right_new)
 
 

time: 139 us -> 143 us (1.029)
  local copies, waits for them, and re-layouts: 6.33 us -> 11.9 us
  Pallas kernels: 127 us -> 124 us
    pallas_call x1, Pallas kernels: 10.2 us -> 5.28 us  [soap_slots(): pl.pallas_call(soap_kernel, out_shape=(f32, jax.ShapeDtypeStruct(gradient...]
    unnamed x3 -> x17, local copies, waits for them, and re-layouts: 3.55 us -> 7.37 us
    pallas_call x1, Pallas kernels: 44.4 us -> 46.7 us  [gather_blocks(): pl.pallas_call(functools.partial(weight_kernel, n_dp, n_chip), out_shape=...]
    gather x1, local copies, waits for them, and re-layouts: 2.08 us -> 3.78 us  [body(): jnp.take(updated, jnp.clip(rank, 0, slot_count - 1), axis=0)]
where the time goes in v7:
time: 143 us
  Pallas kernels  124 us (87%)
  local copies, waits for them, and re-layouts  11.9 us (8%)
  other arithmetic  4.83 us (3%)
  between operations  1.5 us (1%)
    pallas_call x1, Pallas kernels, owned_gradient(): pl.pallas_call(functools.partial(grad_kernel, n_dp, n_chip), out_shape=ja...  72.5 us
    pallas_call x1, Pallas kernels, gather_blocks(): pl.pallas_call(functools.partial(weight_kernel, n_dp, n_chip), out_shape=...  46.7 us
    unnamed x17, local copies, waits for them, and re-layouts  7.37 us
    pallas_call x1, Pallas kernels, soap_slots(): pl.pallas_call(soap_kernel, out_shape=(f32, jax.ShapeDtypeStruct(gradient...  5.28 us
    gather x1, local copies, waits for them, and re-layouts, body(): jnp.take(updated, jnp.clip(rank, 0, slot_count - 1), axis=0)  3.78 us

profile of v7, /device:TPU:1, one launch (start us, length us, event | category | flops | bytes accessed | tf_op | source)
XLA Modules:
  0.0 142.6 jit_solution(2378240107524267780)
XLA Ops:
  1.3 0.9 convert_reduce_fusion.1
  2.2 0.7 compare_and_fusion
  2.9 0.1 broadcast_in_dim.50
  3.0 0.1 copy.24
  3.1 0.1 broadcast_in_dim.46
  3.2 0.1 copy.22
  3.3 0.1 select_reduce_fusion
  3.4 0.1 dynamic-slice_bitcast_fusion.1
  3.5 0.1 compare_convert_fusion
  3.6 0.1 dynamic-slice_convert_fusion
  3.7 0.6 pad_maximum_fusion.scalars
  4.3 0.1 broadcast_bitcast_fusion.1
  4.4 0.1 broadcast_bitcast_fusion
  4.6 1.9 %copy-done.1 = bf16[1,96,128,128]{3,2,1,0:T(8,128)(2,1)S(1)} copy-done((bf16[1,96,128,128]{3,2,1,0:T(8,128)(2,1)S(1)}, bf16[1,96,128,128]{3,2,1,0:T(8,128)(2,1)}, u32[]{:S(2)}) %copy-start.1) | copy-done | bytes 3145752
  6.5 72.5 %shard_map.129 = bf16[768,128]{1,0:T(8,128)(2,1)S(1)} custom-call(s32[2,6]{1,0:T(2,128)S(1)} %pad_add_fusion.sel, bf16[12288,128]{1,0:T(8,128)(2,1)S(1)} %bitcast.15), custom_call_target="tpu_custom_call" | custom-call | tf_op jit(solution)/shard_map/pallas_call | solution.py:255
  79.0 0.8 convert_multiply_fusion.g_ref
  79.8 5.3 %shard_map.130 = (f32[6,128,128]{2,1,0:T(8,128)}, bf16[6,128,128]{2,1,0:T(8,128)(2,1)}) custom-call(f32[7]{0:T(128)} %pad_maximum_fusion.scalars, f32[6,128,128]{2,1,0:T(8,128)} %convert_multiply_fusion.g_ref, f32[6,128,128]{2,1,0:T(8,128)} %m_ref.1, f32[6,128,128]{2,1,0:T(8,128)} %s_ref.1, f32[6,128,128]{2,1,0:T(8,128)} %bl_ref.3, f32[6,128,128]{2,1,0:T(8,128)} %br_ref.3, ...), custom_call_target="tpu_custom_call" | custom-call | tf_op jit(solution)/shard_map/pallas_call | solution.py:338
  85.1 0.0 copy-start.4
  85.1 3.8 %gather_fusion = bf16[96,128,128]{2,1,0:T(8,128)(2,1)} fusion(bf16[6,128,128]{2,1,0:T(8,128)(2,1)} %get-tuple-element.9, s32[1024]{0:T(1024)S(1)} %pad_clamp_fusion), kind=kCustom, calls=%fused_computation | custom fusion | bytes 6291840 | tf_op jit(solution)/shard_map/jit(_take)/gather | solution.py:380
  88.9 1.5 %fusion.1.x_ref = bf16[2,768,128]{2,1,0:T(8,128)(2,1)S(1)} fusion(pred[2,1,768]{2,0,1:T(4,128)(4,1)S(1)} %get-tuple-element.22, pred[2,1,768]{2,0,1:T(4,128)(4,1)S(1)} %get-tuple-element.21, bf16[2,8,768,128]{3,2,1,0:T(8,128)(2,1)} %bitcast.17, s32[]{:T(128)S(6)} %select_n.31), kind=kLoop, calls=%fused_computation.3 | loop fusion | flops 393216 | bytes 789508 | tf_op jit(solution)/shard_map/jit(dynamic_index_in_dim)/squeeze | solution.py:384
  90.5 46.7 %shard_map.131 = (bf16[12288,128]{1,0:T(8,128)(2,1)}, f32[6,128,128]{2,1,0:T(8,128)S(1)}, f32[6,128,128]{2,1,0:T(8,128)S(1)}) custom-call(f32[7]{0:T(128)S(1)} %copy-done.6, bf16[2,768,128]{2,1,0:T(8,128)(2,1)S(1)} %fusion.1.x_ref, f32[6,128,128]{2,1,0:T(8,128)S(1)} %copy-done, f32[6,128,128]{2,1,0:T(8,128)S(1)} %copy-done.4, f32[6,128,128]{2,1,0:T(8,128)S(1)} %copy-done.5, ...), custom_call_target="tpu_custom_call" | custom-call | tf_op jit(solution)/shard_map/pallas_call | solution.py:283
  137.1 4.0 %copy.37 = bf16[96,128,128]{2,1,0:T(8,128)(2,1)} copy(bf16[96,128,128]{2,1,0:T(8,128)(2,1)} %bitcast.18) | data formatting | bytes 6291456
  141.1 0.7 copy.38
  141.9 0.7 copy.39
  (18 shorter events, 0.1 us)
Async XLA Ops:
  4.6 1.9 %copy-start.1 = (bf16[1,96,128,128]{3,2,1,0:T(8,128)(2,1)S(1)}, bf16[1,96,128,128]{3,2,1,0:T(8,128)(2,1)}, u32[]{:S(2)}) copy-start(bf16[1,96,128,128]{3,2,1,0:T(8,128)(2,1)} %param.10) | copy-start | bytes 9437188
  85.1 5.3 %copy-start = (f32[6,128,128]{2,1,0:T(8,128)S(1)}, f32[6,128,128]{2,1,0:T(8,128)}, u32[]{:S(2)}) copy-start(f32[6,128,128]{2,1,0:T(8,128)} %convert_multiply_fusion.g_ref) | copy-start | bytes 1179652
  85.1 5.4 %copy-start.2 = (f32[6,128,128]{2,1,0:T(8,128)S(1)}, f32[6,128,128]{2,1,0:T(8,128)}, u32[]{:S(2)}) copy-start(f32[6,128,128]{2,1,0:T(8,128)} %bl_ref.3) | copy-start | bytes 1179652
  85.1 5.4 %copy-start.3 = (f32[6,128,128]{2,1,0:T(8,128)S(1)}, f32[6,128,128]{2,1,0:T(8,128)}, u32[]{:S(2)}) copy-start(f32[6,128,128]{2,1,0:T(8,128)} %br_ref.3) | copy-start | bytes 1179652
  85.1 5.4 %copy-start.4 = (f32[6,128,128]{2,1,0:T(8,128)S(1)}, f32[6,128,128]{2,1,0:T(8,128)}, u32[]{:S(2)}) copy-start(f32[6,128,128]{2,1,0:T(8,128)} %sl_ref.1) | copy-start | bytes 1179652
  85.1 5.4 %copy-start.5 = (f32[6,128,128]{2,1,0:T(8,128)S(1)}, f32[6,128,128]{2,1,0:T(8,128)}, u32[]{:S(2)}) copy-start(f32[6,128,128]{2,1,0:T(8,128)} %sr_ref.1) | copy-start | bytes 1179652
  85.1 5.4 %copy-start.6 = (f32[7]{0:T(128)S(1)}, f32[7]{0:T(128)}, u32[]{:S(2)}) copy-start(f32[7]{0:T(128)} %pad_maximum_fusion.scalars) | copy-start | bytes 88

commit v8 on v5

--- a/solution.py
+++ b/solution.py
@@ -154,12 +154,16 @@
     return (2, core_me, core_peer), (n_dp, dp_me, dp_peer), (n_chip, chip_me, chip_peer)
 
 
-def grad_kernel(n_dp, n_chip, p_ref, o_ref, buf1, hbuf, buf2, mbuf, buf3, send, recv):
+def grad_kernel(n_dp, n_chip, sel, p_ref, o_ref, buf1, hbuf, buf2, mbuf, buf3, pair, cube, pay, buf5, send, recv):
     core, dp, chip = groups_of(n_dp, n_chip)
     enter((core, dp, chip))
     half = p_ref.shape[0] // 2
     chunk = half // n_dp
     piece = chunk // n_chip
+    rows = cube.shape[1]
+    slots = sel.shape[1]
+    per = chunk // rows
+    share = slots * rows // n_dp
     c, r, m = core[1], dp[1], chip[1]
     finish(phase(core, lambda j: p_ref.at[pl.ds(j * half, half)], lambda me: buf1.at[1], send.at[0], recv.at[0]))
     buf1[0] = p_ref[pl.ds(c * half, half), :]
@@ -169,8 +173,27 @@
     sum_slots(buf2, mbuf, n_dp, chunk, 0)
     buf3[m] = mbuf[pl.ds(m * piece, piece), :]
     finish(phase(chip, lambda j: mbuf.at[pl.ds(j * piece, piece)], lambda me: buf3.at[me], send.at[2], recv.at[2]))
-    sum_slots(buf3, o_ref, n_chip, piece, c * half + r * chunk + m * piece)
-    spread_phases(o_ref, core, dp, chip, piece, send, recv, 3)
+    mine = pair.at[c]
+    sum_slots(buf3, mine, n_chip, piece, m * piece)
+    finish(phase(chip, lambda j: mine.at[pl.ds(m * piece, piece)],
+                 lambda me: mine.at[pl.ds(me * piece, piece)], send.at[3], recv.at[3]))
+    finish(phase(core, lambda j: mine, lambda me: pair.at[me], send.at[4], recv.at[4]))
+    for h in range(2):
+        for i in range(per):
+            cube[h * per + i] = pair[h, pl.ds(i * rows, rows), :]
+    blocks = half // rows
+    for k in range(slots):
+        block = sel[0, k]
+        side = block // blocks
+        within = block - side * blocks
+        inside = (within // per) == r
+        value = cube[side * per + lax.rem(within, per)]
+        pay[pl.ds(k * rows, rows), :] = jnp.where(inside, value, jnp.zeros_like(value))
+    buf5[r] = pay[pl.ds(r * share, share), :]
+    finish(phase(dp, lambda j: pay.at[pl.ds(j * share, share)], lambda me: buf5.at[me], send.at[5], recv.at[5]))
+    sum_slots(buf5, o_ref, n_dp, share, r * share)
+    finish(phase(dp, lambda j: o_ref.at[pl.ds(r * share, share)],
+                 lambda me: o_ref.at[pl.ds(me * share, share)], send.at[6], recv.at[6]))
 
 
 def weight_kernel(n_dp, n_chip, x_ref, o_ref, buf1, pbuf, buf3, send, recv):
@@ -195,8 +218,9 @@
     )
 
 
-def all_reduce_blocks(blocks, n_dp, n_chip):
+def owned_gradient(blocks, sel, n_dp, n_chip):
     count, rows, cols = blocks.shape
+    slots = sel.shape[1]
     flat = blocks.reshape(count * rows, cols)
     half = count * rows // 2
     chunk = half // n_dp
@@ -204,8 +228,8 @@
     vmem = pl.BlockSpec(memory_space=pltpu.VMEM)
     out = pl.pallas_call(
         functools.partial(grad_kernel, n_dp, n_chip),
-        out_shape=jax.ShapeDtypeStruct(flat.shape, flat.dtype),
-        in_specs=[vmem],
+        out_shape=jax.ShapeDtypeStruct((slots * rows, cols), flat.dtype),
+        in_specs=[pl.BlockSpec(memory_space=pltpu.SMEM), vmem],
         out_specs=vmem,
         scratch_shapes=[
             pltpu.VMEM((2, half, cols), flat.dtype),
@@ -213,12 +237,16 @@
             pltpu.VMEM((n_dp, chunk, cols), flat.dtype),
             pltpu.VMEM((chunk, cols), flat.dtype),
             pltpu.VMEM((n_chip, piece, cols), flat.dtype),
-            pltpu.SemaphoreType.DMA((6, n_chip)),
-            pltpu.SemaphoreType.DMA((6, n_chip)),
+            pltpu.VMEM((2, chunk, cols), flat.dtype),
+            pltpu.VMEM((2 * chunk // rows, rows, cols), flat.dtype),
+            pltpu.VMEM((slots * rows, cols), flat.dtype),
+            pltpu.VMEM((n_dp, slots * rows // n_dp, cols), flat.dtype),
+            pltpu.SemaphoreType.DMA((7, n_chip)),
+            pltpu.SemaphoreType.DMA((7, n_chip)),
         ],
         compiler_params=params(0),
-    )(flat)
-    return out.reshape(count, rows, cols)
+    )(sel, flat)
+    return out.reshape(slots, rows, cols)
 
 
 def gather_blocks(chunks, n_dp, n_chip, count):
@@ -320,9 +348,9 @@
     first_slot = lax.axis_index("owner") * slot_count
     occupied_mine = lax.dynamic_slice_in_dim(occupied, first_slot, slot_count, 0)
     source_mine = lax.dynamic_slice_in_dim(source, first_slot, slot_count, 0)
-    grad_sum = all_reduce_blocks(partials[0], n_dp, n_chip)
+    sel = source_mine[None, :].astype(jnp.int32)
     mask_mine = (occupied_mine > 0).astype(jnp.float32)[:, None, None]
-    gradient = jnp.take(grad_sum, source_mine, axis=0).astype(jnp.float32) * mask_mine
+    gradient = owned_gradient(partials[0], sel, n_dp, n_chip).astype(jnp.float32) * mask_mine
     direction, left_new, right_new, updated = soap_slots(
         gradient, occupied_mine, moment, second, stat_left, stat_right, basis_left, basis_right, master, step_count
     )

time: 141 us -> 132 us (0.936)
  Pallas kernels: 130 us -> 120 us
    pallas_call x1, Pallas kernels: 75.4 us -> 63.9 us  [owned_gradient(): pl.pallas_call(functools.partial(grad_kernel, n_dp, n_chip), out_shape=ja...]
    unnamed x1 -> x3, local copies, waits for them, and re-layouts: 1.67 us -> 3.55 us
where the time goes in v8:
time: 132 us
  Pallas kernels  120 us (91%)
  local copies, waits for them, and re-layouts  6.33 us (5%)
  other arithmetic  3.94 us (3%)
  between operations  1.42 us (1%)
    pallas_call x1, Pallas kernels, owned_gradient(): pl.pallas_call(functools.partial(grad_kernel, n_dp, n_chip), out_shape=ja...  63.9 us
    pallas_call x1, Pallas kernels, gather_blocks(): pl.pallas_call(functools.partial(weight_kernel, n_dp, n_chip), out_shape=...  46 us
    pallas_call x1, Pallas kernels, soap_slots(): pl.pallas_call(soap_kernel, out_shape=(f32, f32, f32, jax.ShapeDtypeStruc...  10.2 us
    unnamed x3, local copies, waits for them, and re-layouts  3.55 us

profile of v8, /device:TPU:1, one launch (start us, length us, event | category | flops | bytes accessed | tf_op | source)
XLA Modules:
  0.0 131.8 jit_solution(3926358716513267300)
XLA Ops:
  1.3 0.9 convert_reduce_fusion.1
  2.2 0.7 compare_and_fusion
  2.9 0.1 broadcast_in_dim.53
  3.0 0.1 copy.24
  3.1 0.1 broadcast_in_dim.49
  3.2 0.1 copy.22
  3.3 0.1 select_reduce_fusion
  3.4 0.1 dynamic-slice_bitcast_fusion.sel
  3.5 0.1 compare_convert_fusion
  3.6 0.1 dynamic-slice_convert_fusion
  3.7 0.7 pad_maximum_fusion.scalars
  4.3 0.1 broadcast_bitcast_fusion.1
  4.4 0.1 broadcast_bitcast_fusion
  4.6 0.0 copy-start
  4.6 1.9 %copy-done = bf16[1,96,128,128]{3,2,1,0:T(8,128)(2,1)S(1)} copy-done((bf16[1,96,128,128]{3,2,1,0:T(8,128)(2,1)S(1)}, bf16[1,96,128,128]{3,2,1,0:T(8,128)(2,1)}, u32[]{:S(2)}) %copy-start) | copy-done | bytes 3145752
  6.5 63.9 %shard_map.129 = bf16[768,128]{1,0:T(8,128)(2,1)S(1)} custom-call(s32[1,6]{1,0:T(1,128)S(1)} %dynamic-slice_bitcast_fusion.sel, bf16[12288,128]{1,0:T(8,128)(2,1)S(1)} %bitcast.14), custom_call_target="tpu_custom_call" | custom-call | tf_op jit(solution)/shard_map/pallas_call | solution.py:229
  70.4 0.8 convert_multiply_fusion.g_ref
  71.3 10.2 %shard_map.130 = (f32[6,128,128]{2,1,0:T(8,128)}, f32[6,128,128]{2,1,0:T(8,128)}, f32[6,128,128]{2,1,0:T(8,128)}, bf16[6,128,128]{2,1,0:T(8,128)(2,1)}) custom-call(f32[7]{0:T(128)} %pad_maximum_fusion.scalars, f32[6,128,128]{2,1,0:T(8,128)} %convert_multiply_fusion.g_ref, f32[6,128,128]{2,1,0:T(8,128)} %m_ref.1, f32[6,128,128]{2,1,0:T(8,128)} %s_ref.1, ...), custom_call_target="tpu_custom_call" | custom-call | tf_op jit(solution)/shard_map/pallas_call | solution.py:322
  81.5 2.1 %gather_fusion = bf16[96,128,128]{2,1,0:T(8,128)(2,1)S(1)} fusion(bf16[6,128,128]{2,1,0:T(8,128)(2,1)} %get-tuple-element.8, s32[1024]{0:T(1024)S(1)} %pad_clamp_fusion), kind=kCustom, calls=%fused_computation | custom fusion | bytes 6291840 | tf_op jit(solution)/shard_map/jit(_take)/gather | solution.py:363
  83.6 0.6 fusion.1.x_ref
  84.1 46.0 %shard_map.131 = bf16[12288,128]{1,0:T(8,128)(2,1)S(1)} custom-call(bf16[2,768,128]{2,1,0:T(8,128)(2,1)S(1)} %fusion.1.x_ref), custom_call_target="tpu_custom_call" | custom-call | tf_op jit(solution)/shard_map/pallas_call | solution.py:256
  130.1 1.7 %copy.35 = bf16[96,128,128]{2,1,0:T(8,128)(2,1)} copy(bf16[96,128,128]{2,1,0:T(8,128)(2,1)S(1)} %bitcast.13) | data formatting | bytes 6291456
  (5 shorter events, 0.1 us)
Async XLA Ops:
  4.6 1.9 %copy-start = (bf16[1,96,128,128]{3,2,1,0:T(8,128)(2,1)S(1)}, bf16[1,96,128,128]{3,2,1,0:T(8,128)(2,1)}, u32[]{:S(2)}) copy-start(bf16[1,96,128,128]{3,2,1,0:T(8,128)(2,1)} %param.10) | copy-start | bytes 9437188

commit v9 on v8

--- a/solution.py
+++ b/solution.py
@@ -141,10 +141,27 @@
     base = c * half + r * chunk
     finish(phase(chip, lambda j: o_ref.at[pl.ds(base + m * piece, piece)],
                  lambda me: o_ref.at[pl.ds(base + me * piece, piece)], send.at[first], recv.at[first]))
-    finish(phase(dp, lambda j: o_ref.at[pl.ds(c * half + r * chunk, chunk)],
-                 lambda me: o_ref.at[pl.ds(c * half + me * chunk, chunk)], send.at[first + 1], recv.at[first + 1]))
-    finish(phase(core, lambda j: o_ref.at[pl.ds(c * half, half)],
-                 lambda me: o_ref.at[pl.ds(me * half, half)], send.at[first + 2], recv.at[first + 2]))
+    copies = phase(dp, lambda j: o_ref.at[pl.ds(c * half + r * chunk, chunk)],
+                   lambda me: o_ref.at[pl.ds(c * half + me * chunk, chunk)], send.at[first + 1], recv.at[first + 1])
+    partner = core[2](1 - c)
+    onward = []
+    for k in range(n_dp):
+        if k > 0:
+            copies[k - 1].wait_recv()
+        rows = o_ref.at[pl.ds(c * half + lax.rem(r - k + n_dp, n_dp) * chunk, chunk)]
+        copy = pltpu.make_async_remote_copy(
+            src_ref=rows,
+            dst_ref=rows,
+            send_sem=send.at[first + 2, k],
+            recv_sem=recv.at[first + 2, k],
+            device_id=partner,
+            device_id_type=MESH,
+        )
+        copy.start()
+        onward.append(copy)
+    for copy in copies:
+        copy.wait_send()
+    finish(onward)
 
 
 def groups_of(n_dp, n_chip):

time: 132 us -> 131 us (level)
  no operation moved by 1% of the time
where the time goes in v9:
time: 131 us
  Pallas kernels  119 us (91%)
  local copies, waits for them, and re-layouts  6.33 us (5%)
  other arithmetic  3.94 us (3%)
  between operations  1.42 us (1%)
    pallas_call x1, Pallas kernels, owned_gradient(): pl.pallas_call(functools.partial(grad_kernel, n_dp, n_chip), out_shape=ja...  63.9 us
    pallas_call x1, Pallas kernels, gather_blocks(): pl.pallas_call(functools.partial(weight_kernel, n_dp, n_chip), out_shape=...  44.8 us
    pallas_call x1, Pallas kernels, soap_slots(): pl.pallas_call(soap_kernel, out_shape=(f32, f32, f32, jax.ShapeDtypeStruc...  10.2 us
    unnamed x3, local copies, waits for them, and re-layouts  3.55 us

profile of v9, /device:TPU:1, one launch (start us, length us, event | category | flops | bytes accessed | tf_op | source)
XLA Modules:
  0.0 130.6 jit_solution(2367480350654518592)
XLA Ops:
  1.3 0.9 convert_reduce_fusion.1
  2.2 0.7 compare_and_fusion
  2.9 0.1 broadcast_in_dim.53
  3.0 0.1 copy.24
  3.1 0.1 broadcast_in_dim.49
  3.2 0.1 copy.22
  3.3 0.1 select_reduce_fusion
  3.4 0.1 dynamic-slice_bitcast_fusion.sel
  3.5 0.1 compare_convert_fusion
  3.6 0.1 dynamic-slice_convert_fusion
  3.7 0.7 pad_maximum_fusion.scalars
  4.3 0.1 broadcast_bitcast_fusion.1
  4.4 0.1 broadcast_bitcast_fusion
  4.6 0.0 copy-start
  4.6 1.9 %copy-done = bf16[1,96,128,128]{3,2,1,0:T(8,128)(2,1)S(1)} copy-done((bf16[1,96,128,128]{3,2,1,0:T(8,128)(2,1)S(1)}, bf16[1,96,128,128]{3,2,1,0:T(8,128)(2,1)}, u32[]{:S(2)}) %copy-start) | copy-done | bytes 3145752
  6.5 63.9 %shard_map.129 = bf16[768,128]{1,0:T(8,128)(2,1)S(1)} custom-call(s32[1,6]{1,0:T(1,128)S(1)} %dynamic-slice_bitcast_fusion.sel, bf16[12288,128]{1,0:T(8,128)(2,1)S(1)} %bitcast.14), custom_call_target="tpu_custom_call" | custom-call | tf_op jit(solution)/shard_map/pallas_call | solution.py:246
  70.4 0.8 convert_multiply_fusion.g_ref
  71.3 10.2 %shard_map.130 = (f32[6,128,128]{2,1,0:T(8,128)}, f32[6,128,128]{2,1,0:T(8,128)}, f32[6,128,128]{2,1,0:T(8,128)}, bf16[6,128,128]{2,1,0:T(8,128)(2,1)}) custom-call(f32[7]{0:T(128)} %pad_maximum_fusion.scalars, f32[6,128,128]{2,1,0:T(8,128)} %convert_multiply_fusion.g_ref, f32[6,128,128]{2,1,0:T(8,128)} %m_ref.1, f32[6,128,128]{2,1,0:T(8,128)} %s_ref.1, ...), custom_call_target="tpu_custom_call" | custom-call | tf_op jit(solution)/shard_map/pallas_call | solution.py:339
  81.5 2.1 %gather_fusion = bf16[96,128,128]{2,1,0:T(8,128)(2,1)S(1)} fusion(bf16[6,128,128]{2,1,0:T(8,128)(2,1)} %get-tuple-element.8, s32[1024]{0:T(1024)S(1)} %pad_clamp_fusion), kind=kCustom, calls=%fused_computation | custom fusion | bytes 6291840 | tf_op jit(solution)/shard_map/jit(_take)/gather | solution.py:380
  83.6 0.6 fusion.1.x_ref
  84.1 44.8 %shard_map.131 = bf16[12288,128]{1,0:T(8,128)(2,1)S(1)} custom-call(bf16[2,768,128]{2,1,0:T(8,128)(2,1)S(1)} %fusion.1.x_ref), custom_call_target="tpu_custom_call" | custom-call | tf_op jit(solution)/shard_map/pallas_call | solution.py:273
  128.9 1.7 %copy.35 = bf16[96,128,128]{2,1,0:T(8,128)(2,1)} copy(bf16[96,128,128]{2,1,0:T(8,128)(2,1)S(1)} %bitcast.13) | data formatting | bytes 6291456
  (5 shorter events, 0.1 us)
Async XLA Ops:
  4.6 1.9 %copy-start = (bf16[1,96,128,128]{3,2,1,0:T(8,128)(2,1)S(1)}, bf16[1,96,128,128]{3,2,1,0:T(8,128)(2,1)}, u32[]{:S(2)}) copy-start(bf16[1,96,128,128]{3,2,1,0:T(8,128)(2,1)} %param.10) | copy-start | bytes 9437188

commit v10 on v9

--- a/solution.py
+++ b/solution.py
@@ -182,11 +182,48 @@
     per = chunk // rows
     share = slots * rows // n_dp
     c, r, m = core[1], dp[1], chip[1]
-    finish(phase(core, lambda j: p_ref.at[pl.ds(j * half, half)], lambda me: buf1.at[1], send.at[0], recv.at[0]))
-    buf1[0] = p_ref[pl.ds(c * half, half), :]
-    sum_slots(buf1, hbuf, 2, half, 0)
-    buf2[r] = hbuf[pl.ds(r * chunk, chunk), :]
-    finish(phase(dp, lambda j: hbuf.at[pl.ds(j * chunk, chunk)], lambda me: buf2.at[me], send.at[1], recv.at[1]))
+    partner = core[2](1 - c)
+    order = [lax.rem(r + k, n_dp) for k in range(n_dp)]
+    halves = []
+    for k in range(n_dp):
+        copy = pltpu.make_async_remote_copy(
+            src_ref=p_ref.at[pl.ds((1 - c) * half + order[k] * chunk, chunk)],
+            dst_ref=buf1.at[pl.ds(order[k] * chunk, chunk)],
+            send_sem=send.at[0, k],
+            recv_sem=recv.at[0, k],
+            device_id=partner,
+            device_id_type=MESH,
+        )
+        copy.start()
+        halves.append(copy)
+    onward = []
+    for k in range(n_dp):
+        j = order[k]
+        halves[k].wait_recv()
+        out, start = (buf2.at[r], 0) if k == 0 else (hbuf, j * chunk)
+
+        def add(i, carry, j=j, out=out, start=start):
+            at = pl.multiple_of(i * 128, 128)
+            own = p_ref[pl.ds(c * half + j * chunk + at, 128), :].astype(jnp.float32)
+            got = buf1[pl.ds(j * chunk + at, 128), :].astype(jnp.float32)
+            out[pl.ds(start + at, 128), :] = (own + got).astype(out.dtype)
+            return carry
+
+        lax.fori_loop(0, chunk // 128, add, 0)
+        if k > 0:
+            copy = pltpu.make_async_remote_copy(
+                src_ref=hbuf.at[pl.ds(j * chunk, chunk)],
+                dst_ref=buf2.at[r],
+                send_sem=send.at[1, k],
+                recv_sem=recv.at[1, k],
+                device_id=dp[2](j),
+                device_id_type=MESH,
+            )
+            copy.start()
+            onward.append(copy)
+    for copy in halves:
+        copy.wait_send()
+    finish(onward)
     sum_slots(buf2, mbuf, n_dp, chunk, 0)
     buf3[m] = mbuf[pl.ds(m * piece, piece), :]
     finish(phase(chip, lambda j: mbuf.at[pl.ds(j * piece, piece)], lambda me: buf3.at[me], send.at[2], recv.at[2]))
@@ -249,7 +286,7 @@
         in_specs=[pl.BlockSpec(memory_space=pltpu.SMEM), vmem],
         out_specs=vmem,
         scratch_shapes=[
-            pltpu.VMEM((2, half, cols), flat.dtype),
+            pltpu.VMEM((half, cols), flat.dtype),
             pltpu.VMEM((half, cols), flat.dtype),
             pltpu.VMEM((n_dp, chunk, cols), flat.dtype),
             pltpu.VMEM((chunk, cols), flat.dtype),

time: 131 us -> 128 us (0.977)
  Pallas kernels: 119 us -> 116 us
    pallas_call x1, Pallas kernels: 63.9 us -> 61.6 us  [owned_gradient(): pl.pallas_call(functools.partial(grad_kernel, n_dp, n_chip), out_shape=ja...]
where the time goes in v10:
time: 128 us
  Pallas kernels  116 us (91%)
  local copies, waits for them, and re-layouts  6.33 us (5%)
  other arithmetic  3.94 us (3%)
  between operations  1.42 us (1%)
    pallas_call x1, Pallas kernels, owned_gradient(): pl.pallas_call(functools.partial(grad_kernel, n_dp, n_chip), out_shape=ja...  61.6 us
    pallas_call x1, Pallas kernels, gather_blocks(): pl.pallas_call(functools.partial(weight_kernel, n_dp, n_chip), out_shape=...  44.5 us
    pallas_call x1, Pallas kernels, soap_slots(): pl.pallas_call(soap_kernel, out_shape=(f32, f32, f32, jax.ShapeDtypeStruc...  10.2 us
    unnamed x3, local copies, waits for them, and re-layouts  3.55 us

profile of v10, /device:TPU:1, one launch (start us, length us, event | category | flops | bytes accessed | tf_op | source)
XLA Modules:
  0.0 128.0 jit_solution(15579053018905899367)
XLA Ops:
  1.3 0.9 convert_reduce_fusion.1
  2.2 0.7 compare_and_fusion
  2.9 0.1 broadcast_in_dim.53
  3.0 0.1 copy.24
  3.1 0.1 broadcast_in_dim.49
  3.2 0.1 copy.22
  3.3 0.1 select_reduce_fusion
  3.4 0.1 dynamic-slice_bitcast_fusion.sel
  3.5 0.1 compare_convert_fusion
  3.6 0.1 dynamic-slice_convert_fusion
  3.7 0.7 pad_maximum_fusion.scalars
  4.3 0.1 broadcast_bitcast_fusion.1
  4.4 0.1 broadcast_bitcast_fusion
  4.6 0.0 copy-start
  4.6 1.9 %copy-done = bf16[1,96,128,128]{3,2,1,0:T(8,128)(2,1)S(1)} copy-done((bf16[1,96,128,128]{3,2,1,0:T(8,128)(2,1)S(1)}, bf16[1,96,128,128]{3,2,1,0:T(8,128)(2,1)}, u32[]{:S(2)}) %copy-start) | copy-done | bytes 3145752
  6.5 61.6 %shard_map.129 = bf16[768,128]{1,0:T(8,128)(2,1)S(1)} custom-call(s32[1,6]{1,0:T(1,128)S(1)} %dynamic-slice_bitcast_fusion.sel, bf16[12288,128]{1,0:T(8,128)(2,1)S(1)} %bitcast.14), custom_call_target="tpu_custom_call" | custom-call | tf_op jit(solution)/shard_map/pallas_call | solution.py:283
  68.1 0.8 convert_multiply_fusion.g_ref
  68.9 10.2 %shard_map.130 = (f32[6,128,128]{2,1,0:T(8,128)}, f32[6,128,128]{2,1,0:T(8,128)}, f32[6,128,128]{2,1,0:T(8,128)}, bf16[6,128,128]{2,1,0:T(8,128)(2,1)}) custom-call(f32[7]{0:T(128)} %pad_maximum_fusion.scalars, f32[6,128,128]{2,1,0:T(8,128)} %convert_multiply_fusion.g_ref, f32[6,128,128]{2,1,0:T(8,128)} %m_ref.1, f32[6,128,128]{2,1,0:T(8,128)} %s_ref.1, ...), custom_call_target="tpu_custom_call" | custom-call | tf_op jit(solution)/shard_map/pallas_call | solution.py:376
  79.1 2.1 %gather_fusion = bf16[96,128,128]{2,1,0:T(8,128)(2,1)S(1)} fusion(bf16[6,128,128]{2,1,0:T(8,128)(2,1)} %get-tuple-element.8, s32[1024]{0:T(1024)S(1)} %pad_clamp_fusion), kind=kCustom, calls=%fused_computation | custom fusion | bytes 6291840 | tf_op jit(solution)/shard_map/jit(_take)/gather | solution.py:417
  81.2 0.6 fusion.1.x_ref
  81.8 44.5 %shard_map.131 = bf16[12288,128]{1,0:T(8,128)(2,1)S(1)} custom-call(bf16[2,768,128]{2,1,0:T(8,128)(2,1)S(1)} %fusion.1.x_ref), custom_call_target="tpu_custom_call" | custom-call | tf_op jit(solution)/shard_map/pallas_call | solution.py:310
  126.3 1.7 %copy.35 = bf16[96,128,128]{2,1,0:T(8,128)(2,1)} copy(bf16[96,128,128]{2,1,0:T(8,128)(2,1)S(1)} %bitcast.13) | data formatting | bytes 6291456
  (5 shorter events, 0.1 us)
Async XLA Ops:
  4.6 1.9 %copy-start = (bf16[1,96,128,128]{3,2,1,0:T(8,128)(2,1)S(1)}, bf16[1,96,128,128]{3,2,1,0:T(8,128)(2,1)}, u32[]{:S(2)}) copy-start(bf16[1,96,128,128]{3,2,1,0:T(8,128)(2,1)} %param.10) | copy-start | bytes 9437188

commit v11 on v10

--- a/solution.py
+++ b/solution.py
@@ -334,7 +334,7 @@
     dot = functools.partial(jnp.dot, preferred_element_type=jnp.float32)
     return dot(lh, rh) + (dot(lh, rl) + dot(ll, rh))
 
-def soap_kernel(scalars, g_ref, m_ref, s_ref, sl_ref, sr_ref, bl_ref, br_ref, w_ref, d_out, l_out, r_out, u_out):
+def soap_kernel(scalars, pick, g_ref, m_ref, s_ref, sl_ref, sr_ref, bl_ref, br_ref, w_ref, d_out, l_out, r_out, c_out, u_buf):
     slots = g_ref.shape[0]
     correction = scalars[0]
     chains = []
@@ -351,7 +351,7 @@
         direction = jnp.where(occupied, mm3(basis_left, mm3(scaled, basis_right.T)), 0.0)
         d_out[i] = direction
         master = w_ref[i]
-        u_out[i] = (master - 0.01 * (direction + 0.1 * master)).astype(u_out.dtype)
+        u_buf[i] = (master - 0.01 * (direction + 0.1 * master)).astype(u_buf.dtype)
         left_stat = 0.95 * sl_ref[i] + 0.05 * mm3(gradient, gradient.T)
         right_stat = 0.95 * sr_ref[i] + 0.05 * mm3(gradient.T, gradient)
         chains.append((left_stat, basis_left, l_out, i, occupied))
@@ -366,19 +366,30 @@
         iterates = [1.5 * it - 0.5 * mm3(it, gram) for it, gram in zip(iterates, grams)]
     for (stat, basis, out, i, occupied), it in zip(chains, iterates):
         out[i] = jnp.where(occupied, it, basis)
-
-def soap_slots(gradient, occupied, moment, second, stat_left, stat_right, basis_left, basis_right, master, step_count):
+    halves, rows = c_out.shape[0], g_ref.shape[1]
+    for h in range(halves):
+        for k in range(c_out.shape[1] // rows):
+            index = pick[h * (c_out.shape[1] // rows) + k]
+            value = u_buf[jnp.maximum(index, 0)]
+            c_out[h, pl.ds(k * rows, rows), :] = jnp.where(index >= 0, value, jnp.zeros_like(value))
+
+
+def soap_slots(gradient, occupied, pick, moment, second, stat_left, stat_right, basis_left, basis_right, master, step_count):
+    slots, rows, cols = gradient.shape
     elapsed = step_count[0].astype(jnp.float32)
     correction = 1.0 - jnp.power(jnp.float32(0.95), elapsed)
     scalars = jnp.concatenate([correction[None], occupied.astype(jnp.float32)])
     vmem = pl.BlockSpec(memory_space=pltpu.VMEM)
+    smem = pl.BlockSpec(memory_space=pltpu.SMEM)
     f32 = jax.ShapeDtypeStruct(gradient.shape, jnp.float32)
+    chunks = jax.ShapeDtypeStruct((2, pick.shape[0] // 2 * rows, cols), jnp.bfloat16)
     return pl.pallas_call(
         soap_kernel,
-        out_shape=(f32, f32, f32, jax.ShapeDtypeStruct(gradient.shape, jnp.bfloat16)),
-        in_specs=[pl.BlockSpec(memory_space=pltpu.SMEM)] + [vmem] * 8,
+        out_shape=(f32, f32, f32, chunks),
+        in_specs=[smem, smem] + [vmem] * 8,
         out_specs=(vmem, vmem, vmem, vmem),
-    )(scalars, gradient, moment, second, stat_left, stat_right, basis_left, basis_right, master)
+        scratch_shapes=[pltpu.VMEM(gradient.shape, jnp.bfloat16)],
+    )(scalars, pick, gradient, moment, second, stat_left, stat_right, basis_left, basis_right, master)
 
 
 def body(
@@ -405,20 +416,16 @@
     sel = source_mine[None, :].astype(jnp.int32)
     mask_mine = (occupied_mine > 0).astype(jnp.float32)[:, None, None]
     gradient = owned_gradient(partials[0], sel, n_dp, n_chip).astype(jnp.float32) * mask_mine
-    direction, left_new, right_new, updated = soap_slots(
-        gradient, occupied_mine, moment, second, stat_left, stat_right, basis_left, basis_right, master, step_count
-    )
     block_count = owners.shape[0]
-    count, rows, cols = block_count, updated.shape[1], updated.shape[2]
+    count, rows, cols = block_count, master.shape[1], master.shape[2]
     per = count // (2 * n_dp)
-    rank = target - first_slot
-    in_mine = (rank >= 0) & (rank < slot_count)
-    dense = jnp.where(
-        in_mine[:, None, None], jnp.take(updated, jnp.clip(rank, 0, slot_count - 1), axis=0), 0
-    ).astype(jnp.bfloat16)
     replica = lax.axis_index("dp")
-    chunks = dense.reshape(2, n_dp, per * rows, cols)
-    chunks = lax.dynamic_index_in_dim(chunks, replica, axis=1, keepdims=False)
+    mine = (jnp.arange(2)[:, None] * (count // 2) + replica * per + jnp.arange(per)[None, :]).reshape(-1)
+    rank = jnp.take(target, mine) - first_slot
+    pick = jnp.where((rank >= 0) & (rank < slot_count), rank, -1).astype(jnp.int32)
+    direction, left_new, right_new, chunks = soap_slots(
+        gradient, occupied_mine, pick, moment, second, stat_left, stat_right, basis_left, basis_right, master, step_count
+    )
     weights_all = gather_blocks(chunks, n_dp, n_chip, count).reshape(count, rows, cols)
     return (weights_all, direction, left_new, right_new)
 

time: 128 us -> 127 us (level)
    gather x1, local copies, waits for them, and re-layouts: 2.08 us -> 0.66 us  [body(): rank = jnp.take(target, mine) - first_slot]
    unnamed x3 -> x5, local copies, waits for them, and re-layouts: 3.55 us -> 4.55 us
where the time goes in v11:
time: 127 us
  Pallas kernels  116 us (91%)
  local copies, waits for them, and re-layouts  5.45 us (4%)
  other arithmetic  3.94 us (3%)
  between operations  1.36 us (1%)
    pallas_call x1, Pallas kernels, owned_gradient(): pl.pallas_call(functools.partial(grad_kernel, n_dp, n_chip), out_shape=ja...  61.6 us
    pallas_call x1, Pallas kernels, gather_blocks(): pl.pallas_call(functools.partial(weight_kernel, n_dp, n_chip), out_shape=...  44.2 us
    pallas_call x1, Pallas kernels, soap_slots(): pl.pallas_call(soap_kernel, out_shape=(f32, f32, f32, chunks), in_specs=[...  10.3 us
    unnamed x5, local copies, waits for them, and re-layouts  4.55 us

profile of v11, /device:TPU:1, one launch (start us, length us, event | category | flops | bytes accessed | tf_op | source)
XLA Modules:
  0.0 126.9 jit_solution(4859399718664253082)
XLA Ops:
  1.3 0.1 iota_add_fusion
  1.4 0.1 add.71
  1.5 0.1 add.69
  1.6 0.9 convert_reduce_fusion.1
  2.5 0.7 multiply_add_fusion.1
  3.2 0.1 select_reduce_fusion
  3.3 0.1 dynamic-slice_bitcast_fusion.sel
  3.3 0.1 compare_convert_fusion
  3.4 0.1 dynamic-slice_convert_fusion
  3.5 0.7 pad_maximum_fusion.scalars
  4.2 0.7 gather_fusion
  4.8 0.5 and_select_fusion.pick
  5.3 0.0 copy-start
  5.3 1.9 %copy-done = bf16[1,96,128,128]{3,2,1,0:T(8,128)(2,1)S(1)} copy-done((bf16[1,96,128,128]{3,2,1,0:T(8,128)(2,1)S(1)}, bf16[1,96,128,128]{3,2,1,0:T(8,128)(2,1)}, u32[]{:S(2)}) %copy-start) | copy-done | bytes 3145752
  7.2 61.6 %shard_map.129 = bf16[768,128]{1,0:T(8,128)(2,1)S(1)} custom-call(s32[1,6]{1,0:T(1,128)S(1)} %dynamic-slice_bitcast_fusion.sel, bf16[12288,128]{1,0:T(8,128)(2,1)S(1)} %bitcast.9), custom_call_target="tpu_custom_call" | custom-call | tf_op jit(solution)/shard_map/pallas_call | solution.py:283
  68.8 0.8 convert_multiply_fusion.g_ref
  69.7 10.3 %shard_map.130 = (f32[6,128,128]{2,1,0:T(8,128)}, f32[6,128,128]{2,1,0:T(8,128)}, f32[6,128,128]{2,1,0:T(8,128)}, bf16[2,768,128]{2,1,0:T(8,128)(2,1)}) custom-call(f32[7]{0:T(128)} %pad_maximum_fusion.scalars, s32[12]{0:T(128)} %and_select_fusion.pick, f32[6,128,128]{2,1,0:T(8,128)} %convert_multiply_fusion.g_ref, f32[6,128,128]{2,1,0:T(8,128)} %m_ref.1, ...), custom_call_target="tpu_custom_call" | custom-call | tf_op jit(solution)/shard_map/pallas_call | solution.py:386
  80.0 0.0 copy-start.1
  80.0 1.0 copy-done.1
  81.0 44.2 %shard_map.131 = bf16[12288,128]{1,0:T(8,128)(2,1)S(1)} custom-call(bf16[2,768,128]{2,1,0:T(8,128)(2,1)S(1)} %copy-done.1), custom_call_target="tpu_custom_call" | custom-call | tf_op jit(solution)/shard_map/pallas_call | solution.py:310
  125.2 1.7 %copy.16 = bf16[96,128,128]{2,1,0:T(8,128)(2,1)} copy(bf16[96,128,128]{2,1,0:T(8,128)(2,1)S(1)} %bitcast.8) | data formatting | bytes 6291456
  (3 shorter events, 0.0 us)
Async XLA Ops:
  5.3 1.9 %copy-start = (bf16[1,96,128,128]{3,2,1,0:T(8,128)(2,1)S(1)}, bf16[1,96,128,128]{3,2,1,0:T(8,128)(2,1)}, u32[]{:S(2)}) copy-start(bf16[1,96,128,128]{3,2,1,0:T(8,128)(2,1)} %param.10) | copy-start | bytes 9437188
  80.0 1.0 copy-start.1

commit v12 on v11

--- a/solution.py
+++ b/solution.py
@@ -171,7 +171,7 @@
     return (2, core_me, core_peer), (n_dp, dp_me, dp_peer), (n_chip, chip_me, chip_peer)
 
 
-def grad_kernel(n_dp, n_chip, sel, p_ref, o_ref, buf1, hbuf, buf2, mbuf, buf3, pair, cube, pay, buf5, send, recv):
+def grad_kernel(n_dp, n_chip, sel, p_ref, o_ref, buf1, hbuf, buf2, mbuf, buf3, pair, cube, pay, buf5, own_buf, send, recv, local):
     core, dp, chip = groups_of(n_dp, n_chip)
     enter((core, dp, chip))
     half = p_ref.shape[0] // 2
@@ -196,15 +196,22 @@
         )
         copy.start()
         halves.append(copy)
+    loads = []
+    for k in range(n_dp):
+        rows_at = pl.ds(c * half + order[k] * chunk, chunk)
+        load = pltpu.make_async_copy(p_ref.at[rows_at], own_buf.at[pl.ds(order[k] * chunk, chunk)], local.at[k])
+        load.start()
+        loads.append(load)
     onward = []
     for k in range(n_dp):
         j = order[k]
         halves[k].wait_recv()
+        loads[k].wait()
         out, start = (buf2.at[r], 0) if k == 0 else (hbuf, j * chunk)
 
         def add(i, carry, j=j, out=out, start=start):
             at = pl.multiple_of(i * 128, 128)
-            own = p_ref[pl.ds(c * half + j * chunk + at, 128), :].astype(jnp.float32)
+            own = own_buf[pl.ds(j * chunk + at, 128), :].astype(jnp.float32)
             got = buf1[pl.ds(j * chunk + at, 128), :].astype(jnp.float32)
             out[pl.ds(start + at, 128), :] = (own + got).astype(out.dtype)
             return carry
@@ -283,7 +290,7 @@
     out = pl.pallas_call(
         functools.partial(grad_kernel, n_dp, n_chip),
         out_shape=jax.ShapeDtypeStruct((slots * rows, cols), flat.dtype),
-        in_specs=[pl.BlockSpec(memory_space=pltpu.SMEM), vmem],
+        in_specs=[pl.BlockSpec(memory_space=pltpu.SMEM), pl.BlockSpec(memory_space=pl.ANY)],
         out_specs=vmem,
         scratch_shapes=[
             pltpu.VMEM((half, cols), flat.dtype),
@@ -295,8 +302,10 @@
             pltpu.VMEM((2 * chunk // rows, rows, cols), flat.dtype),
             pltpu.VMEM((slots * rows, cols), flat.dtype),
             pltpu.VMEM((n_dp, slots * rows // n_dp, cols), flat.dtype),
+            pltpu.VMEM((half, cols), flat.dtype),
             pltpu.SemaphoreType.DMA((7, n_chip)),
             pltpu.SemaphoreType.DMA((7, n_chip)),
+            pltpu.SemaphoreType.DMA((n_dp,)),
         ],
         compiler_params=params(0),
     )(sel, flat)

time: 127 us -> 127 us (level)
  no operation moved by 1% of the time
where the time goes in v12:
time: 127 us
  Pallas kernels  116 us (91%)
  local copies, waits for them, and re-layouts  5.45 us (4%)
  other arithmetic  3.94 us (3%)
  between operations  1.36 us (1%)
    pallas_call x1, Pallas kernels, owned_gradient(): pl.pallas_call(functools.partial(grad_kernel, n_dp, n_chip), out_shape=ja...  61.1 us
    pallas_call x1, Pallas kernels, gather_blocks(): pl.pallas_call(functools.partial(weight_kernel, n_dp, n_chip), out_shape=...  44.7 us
    pallas_call x1, Pallas kernels, soap_slots(): pl.pallas_call(soap_kernel, out_shape=(f32, f32, f32, chunks), in_specs=[...  10.3 us
    unnamed x5, local copies, waits for them, and re-layouts  4.55 us

profile of v12, /device:TPU:1, one launch (start us, length us, event | category | flops | bytes accessed | tf_op | source)
XLA Modules:
  0.0 126.9 jit_solution(5090733738050867998)
XLA Ops:
  1.3 0.1 iota_add_fusion
  1.4 0.1 add.71
  1.5 0.1 add.69
  1.6 0.9 convert_reduce_fusion.1
  2.5 0.7 multiply_add_fusion.1
  3.2 0.1 select_reduce_fusion
  3.3 0.1 dynamic-slice_bitcast_fusion.sel
  3.3 0.1 compare_convert_fusion
  3.4 0.1 dynamic-slice_convert_fusion
  3.5 0.7 pad_maximum_fusion.scalars
  4.2 0.7 gather_fusion
  4.8 0.5 and_select_fusion.pick
  5.3 0.0 copy-start
  5.3 1.9 %copy-done = bf16[1,96,128,128]{3,2,1,0:T(8,128)(2,1)S(1)} copy-done((bf16[1,96,128,128]{3,2,1,0:T(8,128)(2,1)S(1)}, bf16[1,96,128,128]{3,2,1,0:T(8,128)(2,1)}, u32[]{:S(2)}) %copy-start) | copy-done | bytes 3145752
  7.2 61.1 %shard_map.129 = bf16[768,128]{1,0:T(8,128)(2,1)S(1)} custom-call(s32[1,6]{1,0:T(1,128)S(1)} %dynamic-slice_bitcast_fusion.sel, bf16[12288,128]{1,0:T(8,128)(2,1)S(1)} %bitcast.9), custom_call_target="tpu_custom_call" | custom-call | tf_op jit(solution)/shard_map/pallas_call | solution.py:290
  68.4 0.8 convert_multiply_fusion.g_ref
  69.2 10.3 %shard_map.130 = (f32[6,128,128]{2,1,0:T(8,128)}, f32[6,128,128]{2,1,0:T(8,128)}, f32[6,128,128]{2,1,0:T(8,128)}, bf16[2,768,128]{2,1,0:T(8,128)(2,1)}) custom-call(f32[7]{0:T(128)} %pad_maximum_fusion.scalars, s32[12]{0:T(128)} %and_select_fusion.pick, f32[6,128,128]{2,1,0:T(8,128)} %convert_multiply_fusion.g_ref, f32[6,128,128]{2,1,0:T(8,128)} %m_ref.1, ...), custom_call_target="tpu_custom_call" | custom-call | tf_op jit(solution)/shard_map/pallas_call | solution.py:395
  79.5 0.0 copy-start.1
  79.5 1.0 copy-done.1
  80.5 44.7 %shard_map.131 = bf16[12288,128]{1,0:T(8,128)(2,1)S(1)} custom-call(bf16[2,768,128]{2,1,0:T(8,128)(2,1)S(1)} %copy-done.1), custom_call_target="tpu_custom_call" | custom-call | tf_op jit(solution)/shard_map/pallas_call | solution.py:319
  125.2 1.7 %copy.16 = bf16[96,128,128]{2,1,0:T(8,128)(2,1)} copy(bf16[96,128,128]{2,1,0:T(8,128)(2,1)S(1)} %bitcast.8) | data formatting | bytes 6291456
  (3 shorter events, 0.0 us)
Async XLA Ops:
  5.3 1.9 %copy-start = (bf16[1,96,128,128]{3,2,1,0:T(8,128)(2,1)S(1)}, bf16[1,96,128,128]{3,2,1,0:T(8,128)(2,1)}, u32[]{:S(2)}) copy-start(bf16[1,96,128,128]{3,2,1,0:T(8,128)(2,1)} %param.10) | copy-start | bytes 9437188
  79.5 1.0 copy-start.1

commit v13 on v11

--- a/solution.py
+++ b/solution.py
@@ -340,7 +340,7 @@
     chains = []
     for i in range(slots):
         occupied = scalars[1 + i] > 0
-        gradient = g_ref[i]
+        gradient = g_ref[i].astype(jnp.float32) * scalars[1 + i]
         basis_left = bl_ref[i]
         basis_right = br_ref[i]
         moment_new = 0.95 * m_ref[i] + 0.05 * gradient
@@ -378,7 +378,7 @@
     slots, rows, cols = gradient.shape
     elapsed = step_count[0].astype(jnp.float32)
     correction = 1.0 - jnp.power(jnp.float32(0.95), elapsed)
-    scalars = jnp.concatenate([correction[None], occupied.astype(jnp.float32)])
+    scalars = jnp.concatenate([correction[None], (occupied > 0).astype(jnp.float32)])
     vmem = pl.BlockSpec(memory_space=pltpu.VMEM)
     smem = pl.BlockSpec(memory_space=pltpu.SMEM)
     f32 = jax.ShapeDtypeStruct(gradient.shape, jnp.float32)
@@ -414,8 +414,7 @@
     occupied_mine = lax.dynamic_slice_in_dim(occupied, first_slot, slot_count, 0)
     source_mine = lax.dynamic_slice_in_dim(source, first_slot, slot_count, 0)
     sel = source_mine[None, :].astype(jnp.int32)
-    mask_mine = (occupied_mine > 0).astype(jnp.float32)[:, None, None]
-    gradient = owned_gradient(partials[0], sel, n_dp, n_chip).astype(jnp.float32) * mask_mine
+    gradient = owned_gradient(partials[0], sel, n_dp, n_chip)
     block_count = owners.shape[0]
     count, rows, cols = block_count, master.shape[1], master.shape[2]
     per = count // (2 * n_dp)

time: 127 us -> 127 us (level)
    unnamed x5 -> x7, local copies, waits for them, and re-layouts: 4.55 us -> 5.21 us
where the time goes in v13:
time: 127 us
  Pallas kernels  116 us (91%)
  local copies, waits for them, and re-layouts  6.11 us (5%)
  other arithmetic  3.04 us (2%)
  between operations  1.37 us (1%)
    pallas_call x1, Pallas kernels, owned_gradient(): pl.pallas_call(functools.partial(grad_kernel, n_dp, n_chip), out_shape=ja...  61.6 us
    pallas_call x1, Pallas kernels, gather_blocks(): pl.pallas_call(functools.partial(weight_kernel, n_dp, n_chip), out_shape=...  44.2 us
    pallas_call x1, Pallas kernels, soap_slots(): pl.pallas_call(soap_kernel, out_shape=(f32, f32, f32, chunks), in_specs=[...  10.2 us
    unnamed x7, local copies, waits for them, and re-layouts  5.21 us

profile of v13, /device:TPU:1, one launch (start us, length us, event | category | flops | bytes accessed | tf_op | source)
XLA Modules:
  0.0 126.6 jit_solution(379836329291336019)
XLA Ops:
  1.3 0.1 iota_add_fusion
  1.4 0.1 add.71
  1.5 0.1 add.69
  1.6 0.9 convert_reduce_fusion.1
  2.5 0.7 multiply_add_fusion.1
  3.2 0.1 select_reduce_fusion
  3.3 0.1 dynamic-slice_bitcast_fusion.sel
  3.3 0.1 compare_convert_fusion
  3.4 0.7 pad_maximum_fusion.scalars
  4.1 0.7 gather_fusion
  4.7 0.6 and_select_fusion.pick
  5.3 0.0 copy-start
  5.3 1.9 %copy-done = bf16[1,96,128,128]{3,2,1,0:T(8,128)(2,1)S(1)} copy-done((bf16[1,96,128,128]{3,2,1,0:T(8,128)(2,1)S(1)}, bf16[1,96,128,128]{3,2,1,0:T(8,128)(2,1)}, u32[]{:S(2)}) %copy-start) | copy-done | bytes 3145752
  7.2 61.6 %shard_map.129 = bf16[768,128]{1,0:T(8,128)(2,1)S(1)} custom-call(s32[1,6]{1,0:T(1,128)S(1)} %dynamic-slice_bitcast_fusion.sel, bf16[12288,128]{1,0:T(8,128)(2,1)S(1)} %bitcast.8), custom_call_target="tpu_custom_call" | custom-call | tf_op jit(solution)/shard_map/pallas_call | solution.py:283
  68.7 0.0 copy-start.1
  68.8 0.7 copy-done.1
  69.4 10.2 %shard_map.130 = (f32[6,128,128]{2,1,0:T(8,128)}, f32[6,128,128]{2,1,0:T(8,128)}, f32[6,128,128]{2,1,0:T(8,128)}, bf16[2,768,128]{2,1,0:T(8,128)(2,1)}) custom-call(f32[7]{0:T(128)} %pad_maximum_fusion.scalars, s32[12]{0:T(128)} %and_select_fusion.pick, bf16[6,128,128]{2,1,0:T(8,128)(2,1)} %bitcast.9, f32[6,128,128]{2,1,0:T(8,128)} %m_ref.1, ...), custom_call_target="tpu_custom_call" | custom-call | tf_op jit(solution)/shard_map/pallas_call | solution.py:386
  79.7 0.0 copy-start.2
  79.7 1.0 copy-done.2
  80.7 44.2 %shard_map.131 = bf16[12288,128]{1,0:T(8,128)(2,1)S(1)} custom-call(bf16[2,768,128]{2,1,0:T(8,128)(2,1)S(1)} %copy-done.2), custom_call_target="tpu_custom_call" | custom-call | tf_op jit(solution)/shard_map/pallas_call | solution.py:310
  124.9 1.7 %copy.16 = bf16[96,128,128]{2,1,0:T(8,128)(2,1)} copy(bf16[96,128,128]{2,1,0:T(8,128)(2,1)S(1)} %bitcast.7) | data formatting | bytes 6291456
  (3 shorter events, 0.0 us)
Async XLA Ops:
  5.3 1.9 %copy-start = (bf16[1,96,128,128]{3,2,1,0:T(8,128)(2,1)S(1)}, bf16[1,96,128,128]{3,2,1,0:T(8,128)(2,1)}, u32[]{:S(2)}) copy-start(bf16[1,96,128,128]{3,2,1,0:T(8,128)(2,1)} %param.10) | copy-start | bytes 9437188
  68.7 0.7 copy-start.1
  79.7 1.0 copy-start.2

commit v14 on v11

--- a/solution.py
+++ b/solution.py
@@ -257,11 +257,43 @@
     piece = chunk // n_chip
     half = n_dp * chunk
     c, r, m = core[1], dp[1], chip[1]
-    finish(phase(core, lambda j: x_ref.at[j], lambda me: buf1.at[1], send.at[0], recv.at[0]))
-    buf1[0] = x_ref[c]
-    sum_slots(buf1, pbuf, 2, chunk, 0)
-    buf3[m] = pbuf[pl.ds(m * piece, piece), :]
-    finish(phase(chip, lambda j: pbuf.at[pl.ds(j * piece, piece)], lambda me: buf3.at[me], send.at[1], recv.at[1]))
+    partner = core[2](1 - c)
+    order = [lax.rem(m + k, n_chip) for k in range(n_chip)]
+    halves = []
+    for k in range(n_chip):
+        copy = pltpu.make_async_remote_copy(
+            src_ref=x_ref.at[1 - c, pl.ds(order[k] * piece, piece)],
+            dst_ref=buf1.at[1, pl.ds(order[k] * piece, piece)],
+            send_sem=send.at[0, k],
+            recv_sem=recv.at[0, k],
+            device_id=partner,
+            device_id_type=MESH,
+        )
+        copy.start()
+        halves.append(copy)
+    onward = []
+    for k in range(n_chip):
+        j = order[k]
+        halves[k].wait_recv()
+        total = x_ref[c, pl.ds(j * piece, piece), :].astype(jnp.float32)
+        total = total + buf1[1, pl.ds(j * piece, piece), :].astype(jnp.float32)
+        if k == 0:
+            buf3[m] = total.astype(buf3.dtype)
+            continue
+        pbuf[pl.ds(j * piece, piece), :] = total.astype(pbuf.dtype)
+        copy = pltpu.make_async_remote_copy(
+            src_ref=pbuf.at[pl.ds(j * piece, piece)],
+            dst_ref=buf3.at[m],
+            send_sem=send.at[1, k],
+            recv_sem=recv.at[1, k],
+            device_id=chip[2](j),
+            device_id_type=MESH,
+        )
+        copy.start()
+        onward.append(copy)
+    for copy in halves:
+        copy.wait_send()
+    finish(onward)
     sum_slots(buf3, o_ref, n_chip, piece, c * half + r * chunk + m * piece)
     spread_phases(o_ref, core, dp, chip, piece, send, recv, 2)
 

time: 127 us -> 128 us (level)
  no operation moved by 1% of the time
where the time goes in v14:
time: 128 us
  Pallas kernels  117 us (91%)
  local copies, waits for them, and re-layouts  5.45 us (4%)
  other arithmetic  3.94 us (3%)
  between operations  1.36 us (1%)
    pallas_call x1, Pallas kernels, owned_gradient(): pl.pallas_call(functools.partial(grad_kernel, n_dp, n_chip), out_shape=ja...  61.6 us
    pallas_call x1, Pallas kernels, gather_blocks(): pl.pallas_call(functools.partial(weight_kernel, n_dp, n_chip), out_shape=...  45.5 us
    pallas_call x1, Pallas kernels, soap_slots(): pl.pallas_call(soap_kernel, out_shape=(f32, f32, f32, chunks), in_specs=[...  10.3 us
    unnamed x5, local copies, waits for them, and re-layouts  4.55 us

profile of v14, /device:TPU:1, one launch (start us, length us, event | category | flops | bytes accessed | tf_op | source)
XLA Modules:
  0.0 128.1 jit_solution(15637136397457537510)
XLA Ops:
  1.3 0.1 iota_add_fusion
  1.4 0.1 add.71
  1.5 0.1 add.69
  1.6 0.9 convert_reduce_fusion.1
  2.5 0.7 multiply_add_fusion.1
  3.2 0.1 select_reduce_fusion
  3.3 0.1 dynamic-slice_bitcast_fusion.sel
  3.3 0.1 compare_convert_fusion
  3.4 0.1 dynamic-slice_convert_fusion
  3.5 0.7 pad_maximum_fusion.scalars
  4.2 0.7 gather_fusion
  4.8 0.5 and_select_fusion.pick
  5.3 0.0 copy-start
  5.3 1.9 %copy-done = bf16[1,96,128,128]{3,2,1,0:T(8,128)(2,1)S(1)} copy-done((bf16[1,96,128,128]{3,2,1,0:T(8,128)(2,1)S(1)}, bf16[1,96,128,128]{3,2,1,0:T(8,128)(2,1)}, u32[]{:S(2)}) %copy-start) | copy-done | bytes 3145752
  7.2 61.6 %shard_map.129 = bf16[768,128]{1,0:T(8,128)(2,1)S(1)} custom-call(s32[1,6]{1,0:T(1,128)S(1)} %dynamic-slice_bitcast_fusion.sel, bf16[12288,128]{1,0:T(8,128)(2,1)S(1)} %bitcast.9), custom_call_target="tpu_custom_call" | custom-call | tf_op jit(solution)/shard_map/pallas_call | solution.py:315
  68.8 0.8 convert_multiply_fusion.g_ref
  69.7 10.3 %shard_map.130 = (f32[6,128,128]{2,1,0:T(8,128)}, f32[6,128,128]{2,1,0:T(8,128)}, f32[6,128,128]{2,1,0:T(8,128)}, bf16[2,768,128]{2,1,0:T(8,128)(2,1)}) custom-call(f32[7]{0:T(128)} %pad_maximum_fusion.scalars, s32[12]{0:T(128)} %and_select_fusion.pick, f32[6,128,128]{2,1,0:T(8,128)} %convert_multiply_fusion.g_ref, f32[6,128,128]{2,1,0:T(8,128)} %m_ref.1, ...), custom_call_target="tpu_custom_call" | custom-call | tf_op jit(solution)/shard_map/pallas_call | solution.py:418
  80.0 0.0 copy-start.1
  80.0 1.0 copy-done.1
  81.0 45.5 %shard_map.131 = bf16[12288,128]{1,0:T(8,128)(2,1)S(1)} custom-call(bf16[2,768,128]{2,1,0:T(8,128)(2,1)S(1)} %copy-done.1), custom_call_target="tpu_custom_call" | custom-call | tf_op jit(solution)/shard_map/pallas_call | solution.py:342
  126.4 1.7 %copy.16 = bf16[96,128,128]{2,1,0:T(8,128)(2,1)} copy(bf16[96,128,128]{2,1,0:T(8,128)(2,1)S(1)} %bitcast.8) | data formatting | bytes 6291456
  (3 shorter events, 0.0 us)
Async XLA Ops:
  5.3 1.9 %copy-start = (bf16[1,96,128,128]{3,2,1,0:T(8,128)(2,1)S(1)}, bf16[1,96,128,128]{3,2,1,0:T(8,128)(2,1)}, u32[]{:S(2)}) copy-start(bf16[1,96,128,128]{3,2,1,0:T(8,128)(2,1)} %param.10) | copy-start | bytes 9437188
  80.0 1.0 copy-start.1

commit v15 on v11

--- a/solution.py
+++ b/solution.py
@@ -98,8 +98,8 @@
 
 def phase(group, source, dest, send, recv):
     n, me, peer = group
-    copies = []
-    for k in range(1, n):
+    copies = {}
+    for k in range(n - 1, 0, -1):
         other = lax.rem(me + k, n)
         copy = pltpu.make_async_remote_copy(
             src_ref=source(other),
@@ -110,8 +110,8 @@
             device_id_type=MESH,
         )
         copy.start()
-        copies.append(copy)
-    return copies
+        copies[k] = copy
+    return [copies[k] for k in range(1, n)]
 
 
 def finish(copies):

time: 127 us -> 131 us (1.031)
  Pallas kernels: 116 us -> 120 us
    pallas_call x1, Pallas kernels: 44.2 us -> 46.7 us  [gather_blocks(): pl.pallas_call(functools.partial(weight_kernel, n_dp, n_chip), out_shape=...]
where the time goes in v15:
time: 131 us; the launch traced here: 130 us
  Pallas kernels  120 us (92%)
  local copies, waits for them, and re-layouts  5.45 us (4%)
  other arithmetic  3.94 us (3%)
  between operations  1.36 us (1%)
    pallas_call x1, Pallas kernels, owned_gradient(): pl.pallas_call(functools.partial(grad_kernel, n_dp, n_chip), out_shape=ja...  62.6 us
    pallas_call x1, Pallas kernels, gather_blocks(): pl.pallas_call(functools.partial(weight_kernel, n_dp, n_chip), out_shape=...  46.7 us
    pallas_call x1, Pallas kernels, soap_slots(): pl.pallas_call(soap_kernel, out_shape=(f32, f32, f32, chunks), in_specs=[...  10.3 us
    unnamed x5, local copies, waits for them, and re-layouts  4.55 us

profile of v15, /device:TPU:1, one launch (start us, length us, event | category | flops | bytes accessed | tf_op | source)
XLA Modules:
  0.0 130.4 jit_solution(12490722897661848380)
XLA Ops:
  1.3 0.1 iota_add_fusion
  1.4 0.1 add.71
  1.5 0.1 add.69
  1.6 0.9 convert_reduce_fusion.1
  2.5 0.7 multiply_add_fusion.1
  3.2 0.1 select_reduce_fusion
  3.3 0.1 dynamic-slice_bitcast_fusion.sel
  3.3 0.1 compare_convert_fusion
  3.4 0.1 dynamic-slice_convert_fusion
  3.5 0.7 pad_maximum_fusion.scalars
  4.2 0.7 gather_fusion
  4.8 0.5 and_select_fusion.pick
  5.3 0.0 copy-start
  5.3 1.9 %copy-done = bf16[1,96,128,128]{3,2,1,0:T(8,128)(2,1)S(1)} copy-done((bf16[1,96,128,128]{3,2,1,0:T(8,128)(2,1)S(1)}, bf16[1,96,128,128]{3,2,1,0:T(8,128)(2,1)}, u32[]{:S(2)}) %copy-start) | copy-done | bytes 3145752
  7.2 62.6 %shard_map.129 = bf16[768,128]{1,0:T(8,128)(2,1)S(1)} custom-call(s32[1,6]{1,0:T(1,128)S(1)} %dynamic-slice_bitcast_fusion.sel, bf16[12288,128]{1,0:T(8,128)(2,1)S(1)} %bitcast.9), custom_call_target="tpu_custom_call" | custom-call | tf_op jit(solution)/shard_map/pallas_call | solution.py:283
  69.9 0.8 convert_multiply_fusion.g_ref
  70.7 10.3 %shard_map.130 = (f32[6,128,128]{2,1,0:T(8,128)}, f32[6,128,128]{2,1,0:T(8,128)}, f32[6,128,128]{2,1,0:T(8,128)}, bf16[2,768,128]{2,1,0:T(8,128)(2,1)}) custom-call(f32[7]{0:T(128)} %pad_maximum_fusion.scalars, s32[12]{0:T(128)} %and_select_fusion.pick, f32[6,128,128]{2,1,0:T(8,128)} %convert_multiply_fusion.g_ref, f32[6,128,128]{2,1,0:T(8,128)} %m_ref.1, ...), custom_call_target="tpu_custom_call" | custom-call | tf_op jit(solution)/shard_map/pallas_call | solution.py:386
  81.0 0.0 copy-start.1
  81.0 1.0 copy-done.1
  82.0 46.7 %shard_map.131 = bf16[12288,128]{1,0:T(8,128)(2,1)S(1)} custom-call(bf16[2,768,128]{2,1,0:T(8,128)(2,1)S(1)} %copy-done.1), custom_call_target="tpu_custom_call" | custom-call | tf_op jit(solution)/shard_map/pallas_call | solution.py:310
  128.7 1.7 %copy.16 = bf16[96,128,128]{2,1,0:T(8,128)(2,1)} copy(bf16[96,128,128]{2,1,0:T(8,128)(2,1)S(1)} %bitcast.8) | data formatting | bytes 6291456
  (3 shorter events, 0.0 us)
Async XLA Ops:
  5.3 1.9 %copy-start = (bf16[1,96,128,128]{3,2,1,0:T(8,128)(2,1)S(1)}, bf16[1,96,128,128]{3,2,1,0:T(8,128)(2,1)}, u32[]{:S(2)}) copy-start(bf16[1,96,128,128]{3,2,1,0:T(8,128)(2,1)} %param.10) | copy-start | bytes 9437188
  81.0 1.0 copy-start.1

commit v16 on v15

--- a/solution.py
+++ b/solution.py
@@ -99,7 +99,8 @@
 def phase(group, source, dest, send, recv):
     n, me, peer = group
     copies = {}
-    for k in range(n - 1, 0, -1):
+    near = [k for pair in zip(range(1, n), range(n - 1, 0, -1)) for k in pair]
+    for k in list(dict.fromkeys(near))[: n - 1]:
         other = lax.rem(me + k, n)
         copy = pltpu.make_async_remote_copy(
             src_ref=source(other),

time: 131 us -> 129 us (0.985)
  Pallas kernels: 120 us -> 118 us
    pallas_call x1, Pallas kernels: 46.7 us -> 45 us  [gather_blocks(): pl.pallas_call(functools.partial(weight_kernel, n_dp, n_chip), out_shape=...]
where the time goes in v16:
time: 129 us
  Pallas kernels  118 us (91%)
  local copies, waits for them, and re-layouts  5.45 us (4%)
  other arithmetic  3.94 us (3%)
  between operations  1.36 us (1%)
    pallas_call x1, Pallas kernels, owned_gradient(): pl.pallas_call(functools.partial(grad_kernel, n_dp, n_chip), out_shape=ja...  62.7 us
    pallas_call x1, Pallas kernels, gather_blocks(): pl.pallas_call(functools.partial(weight_kernel, n_dp, n_chip), out_shape=...  45 us
    pallas_call x1, Pallas kernels, soap_slots(): pl.pallas_call(soap_kernel, out_shape=(f32, f32, f32, chunks), in_specs=[...  10.3 us
    unnamed x5, local copies, waits for them, and re-layouts  4.55 us

profile of v16, /device:TPU:1, one launch (start us, length us, event | category | flops | bytes accessed | tf_op | source)
XLA Modules:
  0.0 128.8 jit_solution(2981834987180764230)
XLA Ops:
  1.3 0.1 iota_add_fusion
  1.4 0.1 add.71
  1.5 0.1 add.69
  1.6 0.9 convert_reduce_fusion.1
  2.5 0.7 multiply_add_fusion.1
  3.2 0.1 select_reduce_fusion
  3.3 0.1 dynamic-slice_bitcast_fusion.sel
  3.3 0.1 compare_convert_fusion
  3.4 0.1 dynamic-slice_convert_fusion
  3.5 0.7 pad_maximum_fusion.scalars
  4.2 0.7 gather_fusion
  4.8 0.5 and_select_fusion.pick
  5.3 0.0 copy-start
  5.3 1.9 %copy-done = bf16[1,96,128,128]{3,2,1,0:T(8,128)(2,1)S(1)} copy-done((bf16[1,96,128,128]{3,2,1,0:T(8,128)(2,1)S(1)}, bf16[1,96,128,128]{3,2,1,0:T(8,128)(2,1)}, u32[]{:S(2)}) %copy-start) | copy-done | bytes 3145752
  7.2 62.7 %shard_map.129 = bf16[768,128]{1,0:T(8,128)(2,1)S(1)} custom-call(s32[1,6]{1,0:T(1,128)S(1)} %dynamic-slice_bitcast_fusion.sel, bf16[12288,128]{1,0:T(8,128)(2,1)S(1)} %bitcast.9), custom_call_target="tpu_custom_call" | custom-call | tf_op jit(solution)/shard_map/pallas_call | solution.py:284
  70.0 0.8 convert_multiply_fusion.g_ref
  70.8 10.3 %shard_map.130 = (f32[6,128,128]{2,1,0:T(8,128)}, f32[6,128,128]{2,1,0:T(8,128)}, f32[6,128,128]{2,1,0:T(8,128)}, bf16[2,768,128]{2,1,0:T(8,128)(2,1)}) custom-call(f32[7]{0:T(128)} %pad_maximum_fusion.scalars, s32[12]{0:T(128)} %and_select_fusion.pick, f32[6,128,128]{2,1,0:T(8,128)} %convert_multiply_fusion.g_ref, f32[6,128,128]{2,1,0:T(8,128)} %m_ref.1, ...), custom_call_target="tpu_custom_call" | custom-call | tf_op jit(solution)/shard_map/pallas_call | solution.py:387
  81.1 0.0 copy-start.1
  81.1 1.0 copy-done.1
  82.1 45.0 %shard_map.131 = bf16[12288,128]{1,0:T(8,128)(2,1)S(1)} custom-call(bf16[2,768,128]{2,1,0:T(8,128)(2,1)S(1)} %copy-done.1), custom_call_target="tpu_custom_call" | custom-call | tf_op jit(solution)/shard_map/pallas_call | solution.py:311
  127.1 1.7 %copy.16 = bf16[96,128,128]{2,1,0:T(8,128)(2,1)} copy(bf16[96,128,128]{2,1,0:T(8,128)(2,1)S(1)} %bitcast.8) | data formatting | bytes 6291456
  (3 shorter events, 0.0 us)
Async XLA Ops:
  5.3 1.9 %copy-start = (bf16[1,96,128,128]{3,2,1,0:T(8,128)(2,1)S(1)}, bf16[1,96,128,128]{3,2,1,0:T(8,128)(2,1)}, u32[]{:S(2)}) copy-start(bf16[1,96,128,128]{3,2,1,0:T(8,128)(2,1)} %param.10) | copy-start | bytes 9437188
  81.1 1.0 copy-start.1
